TPU v7x, 256 devices: a whole 4x4x8 slice. The times are simulated.
256 devices in a mesh: aa: 8 (over x, core), ba: 4 (over y), col: 8 (over z).
Axes of the slice: x: 4, y: 4, z: 8, core: 2. Of those that a mesh axis runs over, the one named last changes fastest.
Arguments:
- r_rows: bfloat16 [131072, 128], P(('aa', 'ba', 'col')), may hold values from -6 to 6
- r_keys: int32 [131072], P(('aa', 'ba', 'col')), may hold values from 0 to 4095
- r_counts: int32 [8192], P(('aa', 'ba', 'col')), may hold values from 0 to 16, as said below
- s_rows: bfloat16 [131072, 128], P(('aa', 'ba', 'col')), may hold values from -6 to 6
- s_keys: int32 [131072], P(('aa', 'ba', 'col')), may hold values from 0 to 4095
- s_counts: int32 [8192], P(('aa', 'ba', 'col')), may hold values from 0 to 16, as said below
- t_rows: bfloat16 [262144, 128], P(('aa', 'ba', 'col')), may hold values from -6 to 6
- t_keys: int32 [262144], P(('aa', 'ba', 'col')), may hold values from 0 to 4095
- t_counts: int32 [16384], P(('aa', 'ba', 'col')), may hold values from 0 to 16, as said below
Outputs:
- joined: bfloat16 [131072, 128], P(('aa', 'ba', 'col'))
Inputs may be any that keep to these rules, and one draw needn't show every extreme that they name: `r_counts`: in every draw one destination pair, drawn from the seed, gets 16 live slots from every device. `s_counts`: in every draw one destination pair, drawn from the seed, gets 16 live slots from every device. `t_counts`: in every draw one destination pair, drawn from the seed, gets 16 live slots from every device.
All inputs are finite; a program needn't handle non-finite values.
Results may differ from a plain program's by a relative error of at most 0.001.
Values may be sent and summed in bfloat16 or wider, within the bound.
A program may use at most 64 MiB of HBM per device.

v0:
```python
import math

import jax
import jax.numpy as jnp
from jax import lax
from jax.sharding import PartitionSpec as P

KEYS = 64
CAP = 16


def packed_total(arrays, axis):
    ends = [0]
    for a in arrays:
        ends.append(ends[-1] + a.size)
    total = lax.psum(jnp.concatenate([a.ravel() for a in arrays]), axis)
    return tuple((total[b:e].reshape(a.shape) for a, b, e in zip(arrays, ends, ends[1:])))


def in_one_piece(arrays, axis, dim, along):
    widths = [math.prod(a.shape[along:]) for a in arrays]
    both = jnp.concatenate(
        [a.reshape(*a.shape[:along], w) for a, w in zip(arrays, widths)], axis=along
    )
    result = lax.psum_scatter(both, axis, scatter_dimension=dim, tiled=True)
    pieces = jnp.split(result, [sum(widths[:k]) for k in range(1, len(widths))], axis=along)
    return tuple(
        (b.reshape(*result.shape[:along], *a.shape[along:]) for a, b in zip(arrays, pieces))
    )


def live_slots(counts):
    place = jnp.arange(CAP, dtype=jnp.int32)
    return (place[None, :] < counts[:, None]).reshape(-1)


def pair_table(keys, rows, live):
    size = KEYS * KEYS
    total = keys.shape[0]
    block = 512
    turns = total // block
    ids = jnp.arange(size, dtype=jnp.int32)

    def add_block(carry, item):
        table, count = carry
        key_block, row_block, live_block = item
        onehot = ((key_block[:, None] == ids[None, :]) & live_block[:, None]).astype(jnp.bfloat16)
        table = table + lax.dot_general(
            onehot, row_block, (((0,), (0,)), ((), ())), preferred_element_type=jnp.float32
        )
        count = count + jnp.sum(onehot, axis=0, dtype=jnp.float32)
        return ((table, count), None)

    start = (jnp.zeros((size, rows.shape[1]), jnp.float32), jnp.zeros((size,), jnp.float32))
    items = (
        keys.reshape(turns, block),
        rows.reshape(turns, block, rows.shape[1]),
        live.reshape(turns, block),
    )
    (table, count), _ = lax.scan(add_block, start, items)
    return (table, count)


def combine(s_table, s_count, t_table, t_count):
    width = s_table.shape[1]
    hi = lax.Precision.HIGHEST
    sd = s_table.reshape(KEYS, KEYS, width)
    scount = s_count.reshape(KEYS, KEYS)
    tu = t_table.reshape(KEYS, KEYS, width)
    tcount = t_count.reshape(KEYS, KEYS)
    total = jnp.einsum("ac,bcw->abw", tcount, sd, precision=hi) + jnp.einsum(
        "bc,acw->abw", scount, tu, precision=hi
    )
    triangles = jnp.einsum("ac,bc->ab", tcount, scount, precision=hi)
    return (total.reshape(KEYS * KEYS, width), triangles.reshape(KEYS * KEYS))


def send_first(rows, keys, counts):
    return (
        lax.all_to_all(rows, ("aa", "ba"), split_axis=0, concat_axis=0, tiled=True),
        lax.all_to_all(keys, ("aa", "ba"), split_axis=0, concat_axis=0, tiled=True),
        lax.all_to_all(counts, ("aa", "ba"), split_axis=0, concat_axis=0, tiled=True),
    )


def send_second(rows, keys, counts):
    return (
        lax.all_to_all(rows, ("ba", "col"), split_axis=0, concat_axis=0, tiled=True),
        lax.all_to_all(keys, ("ba", "col"), split_axis=0, concat_axis=0, tiled=True),
        lax.all_to_all(counts, ("ba", "col"), split_axis=0, concat_axis=0, tiled=True),
    )


def send_third(rows, keys, counts):
    return (
        lax.all_to_all(rows, ("aa", "col"), split_axis=0, concat_axis=0, tiled=True),
        lax.all_to_all(keys, ("aa", "col"), split_axis=0, concat_axis=0, tiled=True),
        lax.all_to_all(counts, ("aa", "col"), split_axis=0, concat_axis=0, tiled=True),
    )


def send_home(joined):
    return lax.all_to_all(joined, ("aa", "ba"), split_axis=0, concat_axis=0, tiled=True)


def body(r_rows, r_keys, r_counts, s_rows, s_keys, s_counts, t_rows, t_keys, t_counts):
    r_held, r_key_held, r_count_held = send_first(r_rows, r_keys, r_counts)
    s_held, s_key_held, s_count_held = send_second(s_rows, s_keys, s_counts)
    t_held, t_key_held, t_count_held = send_third(t_rows, t_keys, t_counts)
    r_live = live_slots(r_count_held)
    r_key_all = lax.all_gather(r_key_held, "col", axis=0, tiled=True)
    s_table, s_count = pair_table(s_key_held, s_held, live_slots(s_count_held))
    s_table, s_count = packed_total((s_table, s_count), "aa")
    t_table, t_count = pair_table(t_key_held, t_held, live_slots(t_count_held))
    t_table, t_count = packed_total((t_table, t_count), "ba")
    total, triangles = combine(s_table, s_count, t_table, t_count)
    rows_total = jnp.take(total, r_key_all, axis=0)
    rows_count = jnp.take(triangles, r_key_all, axis=0)
    mine, counted = in_one_piece((rows_total, rows_count), "col", 0, 1)
    value = r_held.astype(jnp.float32) * mine / jnp.sqrt(1.0 + counted)[:, None]
    joined = jnp.where(r_live[:, None], value, 0.0).astype(jnp.bfloat16)
    return send_home(joined)


def solution(mesh):
    placed = (
        P(("aa", "ba", "col"), None),
        P(("aa", "ba", "col")),
        P(("aa", "ba", "col")),
        P(("aa", "ba", "col"), None),
        P(("aa", "ba", "col")),
        P(("aa", "ba", "col")),
        P(("aa", "ba", "col"), None),
        P(("aa", "ba", "col")),
        P(("aa", "ba", "col")),
    )
    return jax.shard_map(
        body, mesh=mesh, in_specs=placed, out_specs=P(("aa", "ba", "col"), None), check_vma=False
    )
```

profile of v0, /device:TPU:1, one launch (start us, length us, event | category | flops | bytes accessed | tf_op | source)
XLA Modules:
  0.0 377.0 jit_solution(9276544203259005476)
XLA Ops:
  6.5 1.3 copy.32
  7.9 8.6 %all-to-all-start = ((s32[32,1,1]{2,1,0:T(1,128)}), s32[32,1,1]{2,1,0:T(1,128)S(1)}, u32[]{:S(2)}, u32[]{:S(2)}) async-start(s32[32,1,1]{2,1,0:T(1,128)} %copy.32), calls=%async_computation | async-start | bytes 32768 | tf_op jit(solution)/shard_map/all_to_all | solution.py:82
  16.6 1.3 copy.37
  17.9 5.4 %all-to-all-done = s32[32,1,1]{2,1,0:T(1,128)S(1)} async-done(((s32[32,1,1]{2,1,0:T(1,128)}), s32[32,1,1]{2,1,0:T(1,128)S(1)}, u32[]{:S(2)}, u32[]{:S(2)}) %all-to-all-start) | async-done | bytes 160 | tf_op jit(solution)/shard_map/all_to_all | solution.py:82
  23.3 9.1 %all-to-all-start.7 = ((s32[32,1,1]{2,1,0:T(1,128)}), s32[32,1,1]{2,1,0:T(1,128)S(1)}, u32[]{:S(2)}, u32[]{:S(2)}) async-start(s32[32,1,1]{2,1,0:T(1,128)} %copy.37), calls=%async_computation.7 | async-start | bytes 32768 | tf_op jit(solution)/shard_map/all_to_all | solution.py:90
  32.5 1.4 all_to_all.79
  33.8 1.3 copy.35
  35.2 5.9 %all-to-all-done.7 = s32[32,1,1]{2,1,0:T(1,128)S(1)} async-done(((s32[32,1,1]{2,1,0:T(1,128)}), s32[32,1,1]{2,1,0:T(1,128)S(1)}, u32[]{:S(2)}, u32[]{:S(2)}) %all-to-all-start.7) | async-done | bytes 160 | tf_op jit(solution)/shard_map/all_to_all | solution.py:90
  41.1 6.3 %all-to-all-start.4 = ((s32[64,1,1]{2,1,0:T(1,128)}), s32[64,1,1]{2,1,0:T(1,128)S(1)}, u32[]{:S(2)}, u32[]{:S(2)}) async-start(s32[64,1,1]{2,1,0:T(1,128)} %copy.35), calls=%async_computation.4 | async-start | bytes 65536 | tf_op jit(solution)/shard_map/all_to_all | solution.py:98
  47.4 1.4 all_to_all.73
  48.8 0.7 reduce.1
  49.5 0.1 lt.88
  49.6 0.7 reduce.6
  50.3 0.1 lt.99
  50.4 6.3 %all-to-all-done.4 = s32[64,1,1]{2,1,0:T(1,128)S(1)} async-done(((s32[64,1,1]{2,1,0:T(1,128)}), s32[64,1,1]{2,1,0:T(1,128)S(1)}, u32[]{:S(2)}, u32[]{:S(2)}) %all-to-all-start.4) | async-done | bytes 288 | tf_op jit(solution)/shard_map/all_to_all | solution.py:98
  56.7 3.8 %all-to-all-start.6 = ((s32[32,16,1]{1,2,0:T(1,128)}), s32[32,16,1]{1,2,0:T(1,128)S(1)}, u32[]{:S(2)}, u32[]{:S(2)}) async-start(s32[32,16,1]{1,2,0:T(1,128)} %bitcast.10), calls=%async_computation.6 | async-start | bytes 32768 | tf_op jit(solution)/shard_map/all_to_all | solution.py:89
  60.5 1.2 reduce.4
  61.8 0.1 lt.93
  61.9 0.1 lt.95
  62.0 7.2 %all-to-all-done.6 = s32[32,16,1]{1,2,0:T(1,128)S(1)} async-done(((s32[32,16,1]{1,2,0:T(1,128)}), s32[32,16,1]{1,2,0:T(1,128)S(1)}, u32[]{:S(2)}, u32[]{:S(2)}) %all-to-all-start.6) | async-done | bytes 2080 | tf_op jit(solution)/shard_map/all_to_all | solution.py:89
  69.2 6.0 %all-to-all-start.3 = ((s32[64,16,1]{1,2,0:T(1,128)}), s32[64,16,1]{1,2,0:T(1,128)S(1)}, u32[]{:S(2)}, u32[]{:S(2)}) async-start(s32[64,16,1]{1,2,0:T(1,128)} %bitcast.5), calls=%async_computation.3 | async-start | bytes 65536 | tf_op jit(solution)/shard_map/all_to_all | solution.py:97
  75.3 0.5 broadcast.58
  75.7 0.6 reduce.18
  76.4 8.1 %all-to-all-done.3 = s32[64,16,1]{1,2,0:T(1,128)S(1)} async-done(((s32[64,16,1]{1,2,0:T(1,128)}), s32[64,16,1]{1,2,0:T(1,128)S(1)}, u32[]{:S(2)}, u32[]{:S(2)}) %all-to-all-start.3) | async-done | bytes 4128 | tf_op jit(solution)/shard_map/all_to_all | solution.py:97
  84.5 3.9 %all-to-all-start.8 = ((bf16[32,16,128]{2,1,0:T(8,128)(2,1)}), bf16[32,16,128]{2,1,0:T(8,128)(2,1)S(1)}, u32[]{:S(2)}, u32[]{:S(2)}) async-start(bf16[32,16,128]{2,1,0:T(8,128)(2,1)} %bitcast.54), calls=%async_computation.8 | async-start | bytes 262144 | tf_op jit(solution)/shard_map/all_to_all | solution.py:88
  88.3 2.2 convert_reduce_fusion.1
  90.5 0.6 reduce.17
  91.2 0.1 reshape.125
  91.3 6.3 %all-to-all-done.8 = bf16[32,16,128]{2,1,0:T(8,128)(2,1)S(1)} async-done(((bf16[32,16,128]{2,1,0:T(8,128)(2,1)}), bf16[32,16,128]{2,1,0:T(8,128)(2,1)S(1)}, u32[]{:S(2)}, u32[]{:S(2)}) %all-to-all-start.8) | async-done | bytes 131104 | tf_op jit(solution)/shard_map/all_to_all | solution.py:88
  97.6 6.1 %all-to-all-start.5 = ((bf16[64,16,128]{2,1,0:T(8,128)(2,1)}), bf16[64,16,128]{2,1,0:T(8,128)(2,1)S(1)}, u32[]{:S(2)}, u32[]{:S(2)}) async-start(bf16[64,16,128]{2,1,0:T(8,128)(2,1)} %bitcast.50), calls=%async_computation.5 | async-start | bytes 524288 | tf_op jit(solution)/shard_map/all_to_all | solution.py:96
  103.7 0.2 all-reduce.5.cloned.1.call-start
  103.9 2.6 convolution_bitcast_fusion
  106.5 1.4 pad_maximum_fusion.2
  108.0 7.8 %all-to-all-done.5 = bf16[64,16,128]{2,1,0:T(8,128)(2,1)S(1)} async-done(((bf16[64,16,128]{2,1,0:T(8,128)(2,1)}), bf16[64,16,128]{2,1,0:T(8,128)(2,1)S(1)}, u32[]{:S(2)}, u32[]{:S(2)}) %all-to-all-start.5) | async-done | bytes 262176 | tf_op jit(solution)/shard_map/all_to_all | solution.py:96
  115.8 11.5 %while.3 = (s32[]{:T(128)}, f32[4096,128]{1,0:T(8,128)S(1)}, f32[4096]{0:T(1024)S(1)}, s32[2,512]{1,0:T(2,128)S(1)}, pred[2,512]{1,0:T(4,128)(4,1)S(1)}, /*index...) while((s32[]{:T(128)}, f32[4096,128]{1,0:T(8,128)S(1)}, f32[4096]{0:T(1024)S(1)}, ...), condition=%wide.region_2.3_spmd.clone, body=%wide.region_0.2_spmd.clone.sunk | while | flops 552603648 | bytes 4401260 | solution.py:60
  115.8 3.5 fusion.40
  119.2 2.2 convert_reduce_fusion.3
  121.5 3.5 fusion.40
  125.0 2.2 convert_reduce_fusion.3
  127.2 1.5 pad_maximum_fusion.1
  128.8 0.6 copy-done
  129.5 13.1 %all_to_all.99 = s32[32,16,1]{1,2,0:T(1,128)S(1)} all-to-all(s32[32,16,1]{1,2,0:T(1,128)S(1)} %bitcast.57), channel_id=1, replica_groups=mesh['aa'=8,'ba'=4,'col'=8] {'aa','ba'}, dimensions={0} | all-to-all | bytes 4096 | tf_op jit(solution)/shard_map/all_to_all | solution.py:81
  142.6 0.6 reduce.16
  143.3 15.9 %all-gather = s32[8,1,512]{2,1,0:T(1,128)S(1)} all-gather(s32[1,1,512]{2,1,0:T(1,128)S(1)} %reshape.152), channel_id=1, replica_groups=mesh['aa'=8,'ba'=4,'col'=8] {'col'}, dimensions={0}, use_global_device_ids=true | all-gather | bytes 18432 | tf_op jit(solution)/shard_map/all_gather | solution.py:111
  159.2 17.3 %all-reduce.5.cloned.1.call-done = f32[528384]{0:T(1024)} async-done(((f32[528384]{0:T(1024)}), f32[528384]{0:T(1024)}) %all-reduce.5.cloned.1.call-update) | async-done | bytes 2113552 | tf_op jit(solution)/shard_map/psum | solution.py:16
  176.5 0.7 slice.39
  177.4 67.1 %all-reduce.3.cloned.1.call-done = f32[528384]{0:T(1024)} async-done(((f32[528384]{0:T(1024)}), f32[528384]{0:T(1024)}) %all-reduce.3.cloned.1.call-update) | async-done | bytes 2113552 | tf_op jit(solution)/shard_map/psum | solution.py:16
  244.5 0.7 slice.36
  245.3 1.6 slice-done.1
  246.9 2.0 fusion.26
  249.0 3.0 bitcast_add_fusion
  252.0 1.2 copy.39
  253.3 0.2 fusion.27
  253.5 14.1 %gather_fusion = f32[4096,128]{1,0:T(8,128)} fusion(f32[4096,128]{1,0:T(8,128)S(1)} %bitcast.44, s32[4096]{0:T(1024)S(1)} %fusion.24), kind=kCustom, calls=%fused_computation | custom fusion | bytes 4210688 | tf_op jit(solution)/shard_map/jit(_take)/gather | solution.py:117
  267.6 23.0 %gather_fusion.1 = f32[4096]{0:T(1024)S(1)} fusion(f32[4096]{0:T(1024)S(1)} %reshape.132, s32[4096]{0:T(1024)S(1)} %fusion.24), kind=kCustom, calls=%fused_computation.1 | custom fusion | bytes 49152 | tf_op jit(solution)/shard_map/jit(_take)/gather | solution.py:118
  290.7 0.6 copy.40
  291.3 3.6 broadcast_select_fusion
  294.9 2.2 pad_maximum_fusion
  297.2 6.2 %all-to-all-start.1 = ((bf16[32,16,128]{2,1,0:T(8,128)(2,1)}), bf16[32,16,128]{2,1,0:T(8,128)(2,1)S(1)}, u32[]{:S(2)}, u32[]{:S(2)}) async-start(bf16[32,16,128]{2,1,0:T(8,128)(2,1)} %bitcast.1), calls=%async_computation.1 | async-start | bytes 262144 | tf_op jit(solution)/shard_map/all_to_all | solution.py:80
  303.4 49.1 %reduce-scatter.2.cloned.1.call-done = f32[512,129]{1,0:T(8,128)} async-done(((f32[4096,129]{1,0:T(8,128)}), f32[512,129]{1,0:T(8,128)}) %reduce-scatter.2.cloned.1.call-update) | async-done | bytes 264208 | tf_op jit(solution)/shard_map/reduce_scatter | solution.py:25
  352.6 1.1 fusion.20
  353.7 1.2 fusion.23
  354.8 15.0 %all_to_all.100 = bf16[32,16,128]{2,1,0:T(8,128)(2,1)S(1)} all-to-all(bf16[32,16,128]{2,1,0:T(8,128)(2,1)S(1)} %bitcast.48), channel_id=1, replica_groups=mesh['aa'=8,'ba'=4,'col'=8] {'aa','ba'}, dimensions={0} | all-to-all | bytes 262144 | tf_op jit(solution)/shard_map/all_to_all | solution.py:103
  369.8 0.7 copy.54
  (35 shorter events, 1.2 us)
Async XLA Ops:
  7.9 15.5 %all-to-all-start = ((s32[32,1,1]{2,1,0:T(1,128)}), s32[32,1,1]{2,1,0:T(1,128)S(1)}, u32[]{:S(2)}, u32[]{:S(2)}) async-start(s32[32,1,1]{2,1,0:T(1,128)} %copy.32), calls=%async_computation | async-start | bytes 32768 | tf_op jit(solution)/shard_map/all_to_all | solution.py:82
  23.3 17.8 %all-to-all-start.7 = ((s32[32,1,1]{2,1,0:T(1,128)}), s32[32,1,1]{2,1,0:T(1,128)S(1)}, u32[]{:S(2)}, u32[]{:S(2)}) async-start(s32[32,1,1]{2,1,0:T(1,128)} %copy.37), calls=%async_computation.7 | async-start | bytes 32768 | tf_op jit(solution)/shard_map/all_to_all | solution.py:90
  41.1 15.6 %all-to-all-start.4 = ((s32[64,1,1]{2,1,0:T(1,128)}), s32[64,1,1]{2,1,0:T(1,128)S(1)}, u32[]{:S(2)}, u32[]{:S(2)}) async-start(s32[64,1,1]{2,1,0:T(1,128)} %copy.35), calls=%async_computation.4 | async-start | bytes 65536 | tf_op jit(solution)/shard_map/all_to_all | solution.py:98
  56.7 12.5 %all-to-all-start.6 = ((s32[32,16,1]{1,2,0:T(1,128)}), s32[32,16,1]{1,2,0:T(1,128)S(1)}, u32[]{:S(2)}, u32[]{:S(2)}) async-start(s32[32,16,1]{1,2,0:T(1,128)} %bitcast.10), calls=%async_computation.6 | async-start | bytes 32768 | tf_op jit(solution)/shard_map/all_to_all | solution.py:89
  69.2 15.3 %all-to-all-start.3 = ((s32[64,16,1]{1,2,0:T(1,128)}), s32[64,16,1]{1,2,0:T(1,128)S(1)}, u32[]{:S(2)}, u32[]{:S(2)}) async-start(s32[64,16,1]{1,2,0:T(1,128)} %bitcast.5), calls=%async_computation.3 | async-start | bytes 65536 | tf_op jit(solution)/shard_map/all_to_all | solution.py:97
  84.5 13.1 %all-to-all-start.8 = ((bf16[32,16,128]{2,1,0:T(8,128)(2,1)}), bf16[32,16,128]{2,1,0:T(8,128)(2,1)S(1)}, u32[]{:S(2)}, u32[]{:S(2)}) async-start(bf16[32,16,128]{2,1,0:T(8,128)(2,1)} %bitcast.54), calls=%async_computation.8 | async-start | bytes 262144 | tf_op jit(solution)/shard_map/all_to_all | solution.py:88
  97.6 18.2 %all-to-all-start.5 = ((bf16[64,16,128]{2,1,0:T(8,128)(2,1)}), bf16[64,16,128]{2,1,0:T(8,128)(2,1)S(1)}, u32[]{:S(2)}, u32[]{:S(2)}) async-start(bf16[64,16,128]{2,1,0:T(8,128)(2,1)} %bitcast.50), calls=%async_computation.5 | async-start | bytes 524288 | tf_op jit(solution)/shard_map/all_to_all | solution.py:96
  103.7 72.9 %all-reduce.5.cloned.1.call-start = ((), (), s32[]{:S(2)}) async-start(), calls=%async_computation.12 | async-start | bytes 4227072 | tf_op jit(solution)/shard_map/psum | solution.py:16
  107.9 136.6 %all-reduce.3.cloned.1.call-start = ((), (), s32[]{:S(2)}) async-start(), calls=%async_computation.11 | async-start | bytes 4227072 | tf_op jit(solution)/shard_map/psum | solution.py:16
  128.7 0.7 copy-start
  128.7 223.8 %reduce-scatter.2.cloned.1.call-start = ((), (), s32[]{:S(2)}) async-start(), calls=%async_computation.13 | async-start | bytes 4718592 | tf_op jit(solution)/shard_map/reduce_scatter | solution.py:25
  245.3 1.6 slice-start.1
  246.9 2.0 slice-start
  297.2 56.5 %all-to-all-start.1 = ((bf16[32,16,128]{2,1,0:T(8,128)(2,1)}), bf16[32,16,128]{2,1,0:T(8,128)(2,1)S(1)}, u32[]{:S(2)}, u32[]{:S(2)}) async-start(bf16[32,16,128]{2,1,0:T(8,128)(2,1)} %bitcast.1), calls=%async_computation.1 | async-start | bytes 262144 | tf_op jit(solution)/shard_map/all_to_all | solution.py:80
Sparse Core Ops, SparseCore 0:
  108.0 68.4 all-reduce.4
  178.9 65.5 all-reduce.2
  297.3 55.2 reduce-scatter.1
where the time goes:
time: 378 us; the launch traced here: 377 us
  waiting for transfers between devices  181 us (48%)
  local copies, waits for them, and re-layouts  51.9 us (14%)
  starting transfers between devices  50.3 us (13%)
  blocking collectives  44 us (12%)
  other arithmetic  22 us (6%)
  matrix products  14.7 us (4%)
  between operations  13.4 us (4%)
    psum x2, waiting for transfers between devices, packed_total(): total = lax.psum(jnp.concatenate([a.ravel() for a in arrays]), axis)  84.4 us
    reduce_scatter x1, waiting for transfers between devices, in_one_piece(): result = lax.psum_scatter(both, axis, scatter_dimension=dim, tiled=True)  49.1 us
    gather x1, local copies, waits for them, and re-layouts, body(): rows_count = jnp.take(triangles, r_key_all, axis=0)  23 us
    all_gather x1, blocking collectives, body(): r_key_all = lax.all_gather(r_key_held, 'col', axis=0, tiled=True)  15.9 us
    all_to_all x1, blocking collectives, send_home(): lax.all_to_all(joined, ('aa', 'ba'), split_axis=0, concat_axis=0, tiled=T...  15 us
    gather x1, local copies, waits for them, and re-layouts, body(): rows_total = jnp.take(total, r_key_all, axis=0)  14.1 us
    all_to_all x1, blocking collectives, send_first(): lax.all_to_all(keys, ('aa', 'ba'), split_axis=0, concat_axis=0, tiled=True)  13.1 us
    dot_general x3, matrix products, add_block(): lax.dot_general(onehot, row_block, (((0,), (0,)), ((), ())), preferred_el...  9.47 us
  transfers between devices with their start and end apart: 11, of which 10 were waited for; matrix products, arithmetic and copies ran while one was open for 8% of the time, Pallas kernels for 0%

commit v1 on v0

v1 whole, which is shorter than its diff:
```python
import jax
import jax.numpy as jnp
from jax import lax
from jax.experimental import pallas as pl
from jax.experimental.pallas import tpu as pltpu
from jax.sharding import PartitionSpec as P

KEYS = 64
CAP = 16
W = 128
MESH = pl.DeviceIdType.MESH
CHUNK = 512
ROWS_G = 520
F32 = jnp.float32
BF16 = jnp.bfloat16


def place():
    aa = lax.axis_index("aa")
    return lax.div(aa, 2), lax.rem(aa, 2), lax.axis_index("ba"), lax.axis_index("col")


def dev(x, core, y, z):
    return (2 * x + core, y, z)


def dev_s(d, z):
    return dev(lax.div(d, 8), lax.rem(lax.div(d, 4), 2), lax.rem(d, 4), z)


def dev_t(d, x):
    return dev(x, lax.rem(lax.div(d, 4), 2), lax.rem(d, 4), lax.div(d, 8))


def dev_r(d, core, y):
    return dev(lax.rem(d, 4), core, y, lax.div(d, 4))


def greet(barrier, count, me, target):
    def one(t, carry):
        pl.semaphore_signal(
            barrier, inc=1, device_id=target(lax.rem(me + t, count)), device_id_type=MESH
        )
        return carry

    lax.fori_loop(1, count, one, 0)


def drain(ref, sem):
    pltpu.make_async_copy(ref, ref, sem).wait()


def dispatch_kernel(
    s_rows, s_keys, t_rows, t_keys, r_rows, r_keys,
    s_all, sk_all, t_all, tk_all, r_held, rk_all,
    a_send, a_recv, ring_send, ring_recv, t_send, t_recv, k_send, k_recv,
):
    x, core, y, z = place()
    cy = core * 4 + y
    me_s = x * 8 + cy
    me_t = z * 8 + cy
    me_r = z * 4 + x

    barrier = pltpu.get_barrier_semaphore()
    greet(barrier, 32, me_s, lambda d: dev_s(d, z))
    greet(barrier, 64, me_t, lambda d: dev_t(d, x))
    greet(barrier, 32, me_r, lambda d: dev_r(d, core, y))
    pl.semaphore_wait(barrier, 31 + 63 + 31)

    def exchange(count, me, target, pairs):
        for src, dst, n in pairs:
            pltpu.make_async_copy(src.at[me], dst.at[me], a_recv.at[n]).start()

        def one(t, carry):
            d = lax.rem(me + t, count)
            for src, dst, n in pairs:
                pltpu.make_async_remote_copy(
                    src_ref=src.at[d], dst_ref=dst.at[me],
                    send_sem=a_send.at[n], recv_sem=a_recv.at[n],
                    device_id=target(d), device_id_type=MESH,
                ).start()
            return carry

        lax.fori_loop(1, count, one, 0)

    exchange(32, me_s, lambda d: dev_s(d, z), ((s_keys, sk_all.at[z], 1), (s_rows, s_all.at[z], 0)))
    exchange(64, me_t, lambda d: dev_t(d, x), ((t_keys, tk_all.at[x], 3), (t_rows, t_all.at[x], 2)))
    exchange(32, me_r, lambda d: dev_r(d, core, y), ((r_keys, rk_all.at[cy], 5), (r_rows, r_held, 4)))

    def ring(step, way):
        at = lax.rem(z + 8 - way * step, 8)
        target = dev(x, core, y, lax.rem(z + 8 + way, 8))
        lane = 0 if way == 1 else 1
        return [
            pltpu.make_async_remote_copy(
                src_ref=ref.at[at], dst_ref=ref.at[at],
                send_sem=ring_send.at[lane, step, n], recv_sem=ring_recv.at[lane, step, n],
                device_id=target, device_id_type=MESH,
            )
            for n, ref in enumerate((sk_all, s_all))
        ]

    def wait_ring(step, way):
        at = lax.rem(z + 8 - way * (step + 1), 8)
        lane = 0 if way == 1 else 1
        for n, ref in enumerate((sk_all, s_all)):
            drain(ref.at[at], ring_recv.at[lane, step, n])

    started = []

    def go(copies):
        for c in copies:
            c.start()
        started.extend(copies)

    drain(sk_all.at[z], a_recv.at[1])
    drain(s_all.at[z], a_recv.at[0])
    go(ring(0, 1))
    go(ring(0, -1))

    drain(tk_all.at[x], a_recv.at[3])
    drain(t_all.at[x], a_recv.at[2])
    for o in (2, 1, 3):
        go([
            pltpu.make_async_remote_copy(
                src_ref=ref.at[x], dst_ref=ref.at[x],
                send_sem=t_send.at[o - 1, n], recv_sem=t_recv.at[o - 1, n],
                device_id=dev(lax.rem(x + o, 4), core, y, z), device_id_type=MESH,
            )
            for n, ref in enumerate((tk_all, t_all))
        ])

    drain(rk_all.at[cy], a_recv.at[5])
    for o in range(1, 8):
        d = lax.rem(cy + o, 8)
        go([
            pltpu.make_async_remote_copy(
                src_ref=rk_all.at[cy], dst_ref=rk_all.at[cy],
                send_sem=k_send.at[o - 1], recv_sem=k_recv.at[o - 1],
                device_id=dev(x, lax.div(d, 4), lax.rem(d, 4), z), device_id_type=MESH,
            )
        ])

    for step in (0, 1, 2):
        wait_ring(step, 1)
        go(ring(step + 1, 1))
        wait_ring(step, -1)
        if step < 2:
            go(ring(step + 1, -1))
    wait_ring(3, 1)

    drain(r_held, a_recv.at[4])
    for o in range(1, 4):
        at = lax.rem(x + 4 - o, 4)
        for n, ref in enumerate((tk_all, t_all)):
            drain(ref.at[at], t_recv.at[o - 1, n])
    for o in range(1, 8):
        drain(rk_all.at[lax.rem(cy + 8 - o, 8)], k_recv.at[o - 1])

    for n, src in ((0, s_rows), (1, s_keys), (2, t_rows), (3, t_keys), (4, r_rows), (5, r_keys)):
        sent = src.at[pl.ds(0, src.shape[0] - 1)]
        drain(sent, a_send.at[n])
    for c in started:
        c.wait_send()


def dispatch(s_rows, s_keys, t_rows, t_keys, r_rows, r_keys):
    spec = pl.BlockSpec(memory_space=pl.ANY)
    dma = pltpu.SemaphoreType.DMA
    out = (
        jax.ShapeDtypeStruct((8, 32, CAP, W), BF16),
        jax.ShapeDtypeStruct((8, 32, 1, 128), jnp.int32),
        jax.ShapeDtypeStruct((4, 64, CAP, W), BF16),
        jax.ShapeDtypeStruct((4, 64, 1, 128), jnp.int32),
        jax.ShapeDtypeStruct((32, CAP, W), BF16),
        jax.ShapeDtypeStruct((8, 32, 1, 128), jnp.int32),
    )
    return pl.pallas_call(
        dispatch_kernel,
        out_shape=out,
        in_specs=[spec] * 6,
        out_specs=(spec,) * 6,
        scratch_shapes=[
            dma((6,)), dma((6,)),
            dma((2, 4, 2)), dma((2, 4, 2)),
            dma((3, 2)), dma((3, 2)),
            dma((7,)), dma((7,)),
        ],
        compiler_params=pltpu.CompilerParams(collective_id=0, has_side_effects=True),
        name="dispatch",
    )(s_rows, s_keys, t_rows, t_keys, r_rows, r_keys)


def key_lanes(ref, i):
    return jnp.concatenate([ref[pl.ds(4 * i + r, 1), :] for r in range(4)], axis=1) - 1


def hot(values):
    rows = lax.broadcasted_iota(jnp.int32, (KEYS, CHUNK), 0)
    return jnp.where(rows == values, 1.0, 0.0).astype(BF16)


def last_dims(a, b, **kw):
    return lax.dot_general(a, b, (((1,), (1,)), ((), ())), preferred_element_type=F32, **kw)


def split3(v):
    top = v.astype(BF16)
    rest = v - top.astype(F32)
    mid = rest.astype(BF16)
    low = (rest - mid.astype(F32)).astype(BF16)
    return top, mid, low


def join_kernel(idx, sk, tk, rk, s_rows, t_rows, g, acc_s, acc_t, lhs, rhs):
    def count(i, carry):
        sc, tc = carry
        ks, kt = key_lanes(sk, i), key_lanes(tk, i)
        sc = sc + last_dims(hot(ks >> 6), hot(ks & 63))
        tc = tc + last_dims(hot(kt >> 6), hot(kt & 63))
        return sc, tc

    zero = jnp.zeros((KEYS, KEYS), F32)
    sc, tc = lax.fori_loop(0, 8, count, (zero, zero))

    def term(keys, rows, cnt, acc):
        acc[...] = jnp.zeros_like(acc)
        high = jnp.floor(cnt * (1.0 / 256.0)) * 256.0
        parts = jnp.where(jnp.max(cnt) >= 256.0, 2, 1)

        def part(p, carry):
            share = jnp.where(p == 0, cnt - high, high).astype(BF16)

            def chunk(i, carry):
                kv = key_lanes(keys, i)
                first, second = kv >> 6, kv & 63
                seen = jnp.dot(share, hot(second), preferred_element_type=F32)
                outer, inner = first >> 2, (first & 3).astype(F32)
                for h in range(16):
                    mask = jnp.where(outer == h, 1.0, 0.0)
                    lhs[64 * h:64 * h + 64, :] = (seen * mask).astype(BF16)
                for r in range(4):
                    line = inner[:, 128 * r:128 * r + 128]
                    side = jnp.transpose(jnp.broadcast_to(line, (128, 128)))
                    block = rows[pl.ds(pl.multiple_of(CHUNK * i + 128 * r, 128), 128), :].astype(F32)
                    for q in range(4):
                        rhs[128 * r:128 * r + 128, 128 * q:128 * q + 128] = jnp.where(
                            side == float(q), block, 0.0
                        ).astype(BF16)
                for m in range(2):
                    got = jnp.dot(
                        lhs[512 * m:512 * m + 512, :], rhs[...], preferred_element_type=F32
                    )
                    for q in range(4):
                        acc[q, 512 * m:512 * m + 512, :] += got[:, 128 * q:128 * q + 128]
                return carry

            return lax.fori_loop(0, 8, chunk, carry)

        lax.fori_loop(0, parts, part, 0)

    term(sk, s_rows, tc, acc_s)
    term(tk, t_rows, sc, acc_t)

    tri = last_dims(sc, tc, precision=lax.Precision.HIGHEST)
    stack = jnp.concatenate(split3(tri), axis=1)

    def gather(o, carry):
        kv = key_lanes(rk, o)
        first = hot(kv >> 6)
        sums = jnp.dot(
            stack, jnp.concatenate([first, first, first], axis=0), preferred_element_type=F32
        )
        line = jnp.sum(sums * hot(kv & 63).astype(F32), axis=0, keepdims=True)
        for r in range(4):
            g[o, 512 + r:513 + r, :] = line[:, 128 * r:128 * r + 128]
        g[o, 516:520, :] = jnp.zeros((4, 128), F32)

        def eight(i, carry):
            for u in range(8):
                at = idx[o * 512 + i * 8 + u]
                one, two = at & 4095, at >> 12
                g[o, pl.ds(i * 8 + u, 1), :] = (
                    acc_s[two_part(one), pl.ds(one & 1023, 1), :]
                    + acc_t[two_part(two), pl.ds(two & 1023, 1), :]
                )
            return carry

        return lax.fori_loop(0, 64, eight, carry)

    def two_part(v):
        return v >> 10

    lax.fori_loop(0, 8, gather, 0)


def join(idx, sk, tk, rk, s_rows, t_rows):
    vm = pl.BlockSpec(memory_space=pltpu.VMEM)
    return pl.pallas_call(
        join_kernel,
        out_shape=jax.ShapeDtypeStruct((8, ROWS_G, W), F32),
        in_specs=[pl.BlockSpec(memory_space=pltpu.SMEM)] + [vm] * 5,
        out_specs=vm,
        scratch_shapes=[
            pltpu.VMEM((4, 1024, W), F32),
            pltpu.VMEM((4, 1024, W), F32),
            pltpu.VMEM((1024, CHUNK), BF16),
            pltpu.VMEM((CHUNK, 4 * W), BF16),
        ],
        compiler_params=pltpu.CompilerParams(vmem_limit_bytes=40 << 20),
        name="join",
    )(idx, sk, tk, rk, s_rows, t_rows)


def finish_kernel(g, rows, keys, out, ra, rb, h, joined, sems, p_send, p_recv, y_send, y_recv):
    x, core, y, z = place()
    me_r = z * 4 + x
    barrier = pltpu.get_barrier_semaphore()
    pl.semaphore_signal(barrier, inc=1, device_id=dev(x, 1 - core, y, z), device_id_type=MESH)
    for o in (1, 2, 3):
        pl.semaphore_signal(
            barrier, inc=1, device_id=dev(x, core, lax.rem(y + o, 4), z), device_id_type=MESH
        )
    greet(barrier, 32, me_r, lambda d: dev_r(d, core, y))
    pl.semaphore_wait(barrier, 1 + 3 + 31)

    order = (2, 1, 3, 0)
    partner = []
    for o in order:
        c = pltpu.make_async_remote_copy(
            src_ref=g.at[(1 - core) * 4 + lax.rem(y + o, 4)], dst_ref=ra.at[o],
            send_sem=p_send.at[o], recv_sem=p_recv.at[o],
            device_id=dev(x, 1 - core, y, z), device_id_type=MESH,
        )
        c.start()
        partner.append(c)
    sent = []
    for n, o in enumerate(order):
        partner[n].wait_recv()
        to = lax.rem(y + o, 4)
        h[o] = g[core * 4 + to] + ra[o]
        if o:
            c = pltpu.make_async_remote_copy(
                src_ref=h.at[o], dst_ref=rb.at[o - 1],
                send_sem=y_send.at[o - 1], recv_sem=y_recv.at[o - 1],
                device_id=dev(x, core, to, z), device_id_type=MESH,
            )
            c.start()
            sent.append(c)
    for c in sent:
        c.wait_recv()
    line = h[0, 512:520, :] + rb[0, 512:520, :] + rb[1, 512:520, :] + rb[2, 512:520, :]
    scale = jnp.where(keys[...] > 0, 1.0 / jnp.sqrt(1.0 + line), 0.0)
    for r in range(4):
        at = pl.ds(128 * r, 128)
        side = jnp.transpose(jnp.broadcast_to(scale[r:r + 1, :], (128, 128)))
        total = h[0, at, :] + rb[0, at, :] + rb[1, at, :] + rb[2, at, :]
        value = rows[at, :].astype(F32) * total * side
        joined[8 * r:8 * r + 8] = value.astype(BF16).reshape(8, CAP, W)

    pltpu.make_async_copy(joined.at[me_r], out.at[me_r], sems.at[1]).start()

    def home(t, carry):
        d = lax.rem(me_r + t, 32)
        pltpu.make_async_remote_copy(
            src_ref=joined.at[d], dst_ref=out.at[me_r],
            send_sem=sems.at[0], recv_sem=sems.at[1],
            device_id=dev_r(d, core, y), device_id_type=MESH,
        ).start()
        return carry

    lax.fori_loop(1, 32, home, 0)
    drain(out, sems.at[1])
    drain(joined.at[pl.ds(0, 31)], sems.at[0])
    for c in partner + sent:
        c.wait_send()


def finish(g, rows, keys):
    vm = pl.BlockSpec(memory_space=pltpu.VMEM)
    dma = pltpu.SemaphoreType.DMA
    return pl.pallas_call(
        finish_kernel,
        out_shape=jax.ShapeDtypeStruct((32, CAP, W), BF16),
        in_specs=[vm] * 3,
        out_specs=pl.BlockSpec(memory_space=pl.ANY),
        scratch_shapes=[
            pltpu.VMEM((4, ROWS_G, W), F32),
            pltpu.VMEM((3, ROWS_G, W), F32),
            pltpu.VMEM((4, ROWS_G, W), F32),
            pltpu.VMEM((32, CAP, W), BF16),
            dma((2,)), dma((4,)), dma((4,)), dma((3,)), dma((3,)),
        ],
        compiler_params=pltpu.CompilerParams(
            collective_id=1, has_side_effects=True, vmem_limit_bytes=40 << 20
        ),
        name="finish",
    )(g, rows, keys)


def lay_keys(keys, counts, seat):
    groups = counts.shape[0]
    spot = lax.broadcasted_iota(jnp.int32, (groups, CAP), 1)
    live = jnp.where(spot < counts[:, None], keys.reshape(groups, CAP) + 1, 0)
    lane = lax.broadcasted_iota(jnp.int32, (groups, 128), 1)
    wide = jnp.where(lane // CAP == seat, jnp.tile(live, (1, 8)), 0)
    return wide.reshape(groups, 1, 128)


def body(r_rows, r_keys, r_counts, s_rows, s_keys, s_counts, t_rows, t_keys, t_counts):
    x, core, y, z = place()
    cy = core * 4 + y
    s_all, sk_all, t_all, tk_all, r_held, rk_all = dispatch(
        s_rows.reshape(32, CAP, W), lay_keys(s_keys, s_counts, cy),
        t_rows.reshape(64, CAP, W), lay_keys(t_keys, t_counts, cy),
        r_rows.reshape(32, CAP, W), lay_keys(r_keys, r_counts, (z * 4 + x) % 8),
    )
    sk = jnp.sum(sk_all.reshape(32, 8, 128), axis=1)
    tk = jnp.sum(tk_all.reshape(32, 8, 128), axis=1)
    rk = jnp.sum(rk_all.reshape(32, 8, 128), axis=1)
    kv = jnp.maximum(rk - 1, 0)
    a, b = kv >> 6, kv & 63
    at_s = (b & 3) * 1024 + (b >> 2) * 64 + a
    at_t = (a & 3) * 1024 + (a >> 2) * 64 + b
    idx = (at_s + at_t * 4096).reshape(4096)
    g = join(idx, sk, tk, rk, s_all.reshape(4096, W), t_all.reshape(4096, W))
    own = lax.dynamic_slice(rk, (cy * 4, 0), (4, 128))
    own = jnp.concatenate([own, jnp.zeros((4, 128), jnp.int32)], axis=0)
    joined = finish(g, r_held.reshape(512, W), own)
    return joined.reshape(512, W)


def solution(mesh):
    rows, line = P(("aa", "ba", "col"), None), P(("aa", "ba", "col"))
    return jax.shard_map(
        body, mesh=mesh, in_specs=(rows, line, line) * 3, out_specs=rows, check_vma=False
    )
```

time: 378 us -> 121 us (0.32)
  waiting for transfers between devices: 181 us -> 0 us
  Pallas kernels: 0 us -> 109 us
  starting transfers between devices: 50.3 us -> 0 us
  local copies, waits for them, and re-layouts: 51.9 us -> 3.76 us
  blocking collectives: 44 us -> 0 us
  matrix products: 14.7 us -> 0 us
  other arithmetic: 22 us -> 8.46 us
  between operations: 13.4 us -> 0.09 us
    pallas_call x0 -> x3, Pallas kernels: none -> 109 us  [the longest x1 41.9 us: dispatch(): pl.pallas_call(dispatch_kernel, out_shape=out, in_specs=[spec] * 6, out_s...]
    psum x2 -> x0, waiting for transfers between devices: 84.4 us -> none  [packed_total(): total = lax.psum(jnp.concatenate([a.ravel() for a in arrays]), axis)]
    all_to_all x8 -> x0, starting transfers between devices: 50 us -> none  [the longest x1 9.14 us: send_second(): lax.all_to_all(counts, ('ba', 'col'), split_axis=0, concat_axis=0, tiled=...]
    reduce_scatter x1 -> x0, waiting for transfers between devices: 49.1 us -> none  [in_one_piece(): result = lax.psum_scatter(both, axis, scatter_dimension=dim, tiled=True)]
    all_to_all x8 -> x0, waiting for transfers between devices: 47 us -> none  [the longest x1 8.06 us: send_third(): lax.all_to_all(keys, ('aa', 'col'), split_axis=0, concat_axis=0, tiled=True)]
    gather x2 -> x0, local copies, waits for them, and re-layouts: 37.1 us -> none  [the longest x1 23 us: body(): rows_count = jnp.take(triangles, r_key_all, axis=0)]
    all_to_all x2 -> x0, blocking collectives: 28.1 us -> none  [the longest x1 15 us: send_home(): lax.all_to_all(joined, ('aa', 'ba'), split_axis=0, concat_axis=0, tiled=T...]
    all_gather x1 -> x0, blocking collectives: 15.9 us -> none  [body(): r_key_all = lax.all_gather(r_key_held, 'col', axis=0, tiled=True)]
  transfers between devices with their start and end apart: 11 -> 0, of which waited for: 10 -> 0; matrix products, arithmetic and copies ran while one was open for 8% -> 0% of each run, Pallas kernels for 0% -> 0%
where the time goes in v1:
time: 121 us
  Pallas kernels  109 us (90%)
  other arithmetic  8.46 us (7%)
  local copies, waits for them, and re-layouts  3.76 us (3%)
    pallas_call x1, Pallas kernels, dispatch(): pl.pallas_call(dispatch_kernel, out_shape=out, in_specs=[spec] * 6, out_s...  41.9 us
    pallas_call x1, Pallas kernels, join(): pl.pallas_call(join_kernel, out_shape=jax.ShapeDtypeStruct((8, ROWS_G, W)...  36.8 us
    pallas_call x1, Pallas kernels, finish(): pl.pallas_call(finish_kernel, out_shape=jax.ShapeDtypeStruct((32, CAP, W)...  29.8 us
    unnamed x7, local copies, waits for them, and re-layouts  3.1 us

profile of v1, /device:TPU:1, one launch (start us, length us, event | category | flops | bytes accessed | tf_op | source)
XLA Modules:
  0.0 120.9 jit_solution(2546085609332593262)
XLA Ops:
  0.0 0.7 broadcast_add_fusion.2
  0.7 0.1 add.77
  0.8 0.7 fusion.10
  1.5 0.1 copy.10
  1.6 0.1 copy.11
  1.6 0.7 broadcast_add_fusion.1
  2.4 0.1 add.84
  2.4 0.7 fusion.11
  3.2 0.1 copy.14
  3.2 0.1 copy.15
  3.3 0.7 compare_select_fusion.1
  4.0 0.7 broadcast_add_fusion
  4.7 0.1 add.80
  4.7 0.7 fusion
  5.5 0.1 copy.12
  5.5 0.1 copy.13
  5.6 0.7 compare_select_fusion.t_keys
  6.3 41.9 %dispatch.1 = (bf16[8,32,16,128]{3,2,1,0:T(8,128)(2,1)}, s32[8,32,1,128]{3,2,1,0:T(1,128)}, bf16[4,64,16,128]{3,2,1,0:T(8,128)(2,1)}, s32[4,64,1,128]{3,2,1,0:T(...) custom-call(bf16[32,16,128]{2,1,0:T(8,128)(2,1)} %bitcast.58, s32[32,1,128]{2,1,0:T(1,128)} %get-tuple-element.18.s_keys, ...), custom_call_target="tpu_custom_call" | custom-call | tf_op jit(solution)/shard_map/dispatch/pallas_call | solution.py:178
  48.2 0.9 reduce_sum.27.rk
  49.2 0.9 reduce_sum.28.sk
  50.1 0.9 reduce_sum.29.tk
  51.1 0.0 copy-start
  51.1 1.2 %copy-done = bf16[8,32,16,128]{3,2,1,0:T(8,128)(2,1)S(1)} copy-done((bf16[8,32,16,128]{3,2,1,0:T(8,128)(2,1)S(1)}, bf16[8,32,16,128]{3,2,1,0:T(8,128)(2,1)}, u32[]{:S(2)}) %copy-start) | copy-done | bytes 1048600
  52.3 0.0 copy-start.1
  52.3 1.2 %copy-done.1 = bf16[4,64,16,128]{3,2,1,0:T(8,128)(2,1)S(1)} copy-done((bf16[4,64,16,128]{3,2,1,0:T(8,128)(2,1)S(1)}, bf16[4,64,16,128]{3,2,1,0:T(8,128)(2,1)}, u32[]{:S(2)}) %copy-start.1) | copy-done | bytes 1048600
  53.5 0.0 copy-start.2
  53.5 36.8 %join.1.g = f32[8,520,128]{2,1,0:T(8,128)S(1)} custom-call(s32[4096]{0:T(1024)S(1)} %fusion.1.idx, s32[32,128]{1,0:T(8,128)S(1)} %reduce_sum.28.sk, s32[32,128]{1,0:T(8,128)S(1)} %reduce_sum.29.tk, s32[32,128]{1,0:T(8,128)S(1)} %reduce_sum.27.rk, bf16[4096,128]{1,0:T(8,128)(2,1)S(1)} %bitcast.47, bf16[4096,128]{1,0:T(8,128)(2,1)S(1)} %bitcast.48), custom_call_target="tpu_custom_call" | custom-call | tf_op jit(solution)/shard_map/join/pallas_call | solution.py:299
  90.4 0.0 copy-done.2
  90.4 29.8 %finish.1 = bf16[32,16,128]{2,1,0:T(8,128)(2,1)S(1)} custom-call(f32[8,520,128]{2,1,0:T(8,128)S(1)} %join.1.g, bf16[512,128]{1,0:T(8,128)(2,1)S(1)} %bitcast.50, s32[8,128]{1,0:T(8,128)S(1)} %concatenate.3.keys), custom_call_target="tpu_custom_call" | custom-call | tf_op jit(solution)/shard_map/finish/pallas_call | solution.py:382
  120.2 0.7 copy.17
  (8 shorter events, 0.1 us)
Async XLA Ops:
  51.1 1.2 %copy-start = (bf16[8,32,16,128]{3,2,1,0:T(8,128)(2,1)S(1)}, bf16[8,32,16,128]{3,2,1,0:T(8,128)(2,1)}, u32[]{:S(2)}) copy-start(bf16[8,32,16,128]{3,2,1,0:T(8,128)(2,1)} %get-tuple-element.14) | copy-start | bytes 3145732
  52.3 1.2 %copy-start.1 = (bf16[4,64,16,128]{3,2,1,0:T(8,128)(2,1)S(1)}, bf16[4,64,16,128]{3,2,1,0:T(8,128)(2,1)}, u32[]{:S(2)}) copy-start(bf16[4,64,16,128]{3,2,1,0:T(8,128)(2,1)} %get-tuple-element.15) | copy-start | bytes 3145732
  53.5 36.9 %copy-start.2 = (bf16[32,16,128]{2,1,0:T(8,128)(2,1)S(1)}, bf16[32,16,128]{2,1,0:T(8,128)(2,1)}, u32[]{:S(2)}) copy-start(bf16[32,16,128]{2,1,0:T(8,128)(2,1)} %get-tuple-element.16) | copy-start | bytes 393220

commit v2 on v0

v2 whole, which is shorter than its diff:
```python
import jax
import jax.numpy as jnp
from jax import lax
from jax.experimental import pallas as pl
from jax.experimental.pallas import tpu as pltpu
from jax.sharding import PartitionSpec as P

KEYS = 64
CAP = 16
W = 128
MESH = pl.DeviceIdType.MESH
CHUNK = 512
ROWS_G = 520
F32 = jnp.float32
BF16 = jnp.bfloat16


def place():
    aa = lax.axis_index("aa")
    return lax.div(aa, 2), lax.rem(aa, 2), lax.axis_index("ba"), lax.axis_index("col")


def dev(x, core, y, z):
    return (2 * x + core, y, z)


def dev_s(d, z):
    return dev(lax.div(d, 8), lax.rem(lax.div(d, 4), 2), lax.rem(d, 4), z)


def dev_t(d, x):
    return dev(x, lax.rem(lax.div(d, 4), 2), lax.rem(d, 4), lax.div(d, 8))


def dev_r(d, core, y):
    return dev(lax.rem(d, 4), core, y, lax.div(d, 4))


def greet(barrier, count, me, target):
    def one(t, carry):
        pl.semaphore_signal(
            barrier, inc=1, device_id=target(lax.rem(me + t, count)), device_id_type=MESH
        )
        return carry

    lax.fori_loop(1, count, one, 0)


def drain(ref, sem):
    pltpu.make_async_copy(ref, ref, sem).wait()


def push(src, dst, send, recv, target):
    copy = pltpu.make_async_remote_copy(
        src_ref=src, dst_ref=dst, send_sem=send, recv_sem=recv,
        device_id=target, device_id_type=MESH,
    )
    copy.start()
    return copy


def hot(values):
    rows = lax.broadcasted_iota(jnp.int32, (KEYS, CHUNK), 0)
    return jnp.where(rows == values, 1.0, 0.0).astype(BF16)


def last_dims(a, b, **kw):
    return lax.dot_general(a, b, (((1,), (1,)), ((), ())), preferred_element_type=F32, **kw)


def split3(v):
    top = v.astype(BF16)
    rest = v - top.astype(F32)
    mid = rest.astype(BF16)
    low = (rest - mid.astype(F32)).astype(BF16)
    return top, mid, low


def key_line(ref, block, row):
    return jnp.concatenate([ref[block, row + r:row + r + 1, :] for r in range(4)], axis=1) - 1


def product(kv, share, load, acc, lhs, rhs):
    first, second = kv >> 6, kv & 63
    seen = jnp.dot(share, hot(second), preferred_element_type=F32)
    outer, inner = first >> 2, (first & 3).astype(F32)
    for h in range(16):
        mask = jnp.where(outer == h, 1.0, 0.0)
        lhs[64 * h:64 * h + 64, :] = (seen * mask).astype(BF16)
    for r in range(4):
        side = jnp.transpose(jnp.broadcast_to(inner[:, 128 * r:128 * r + 128], (128, 128)))
        block = load(r).astype(F32)
        for q in range(4):
            rhs[128 * r:128 * r + 128, 128 * q:128 * q + 128] = jnp.where(
                side == float(q), block, 0.0
            ).astype(BF16)
    for m in range(2):
        got = jnp.dot(lhs[512 * m:512 * m + 512, :], rhs[...], preferred_element_type=F32)
        for q in range(4):
            at = 1024 * q + 512 * m
            acc[at:at + 512, :] += got[:, 128 * q:128 * q + 128]


def live_keys(keys, counts):
    rows, groups = keys.shape[0], counts.shape[1]
    row = lax.broadcasted_iota(jnp.int32, (rows, groups), 0)
    group = lax.broadcasted_iota(jnp.int32, (rows, groups), 1)
    spread = jnp.where(group // 8 == row, counts.astype(F32), 0.0).astype(BF16)
    group = lax.broadcasted_iota(jnp.int32, (groups, 128), 0)
    lane = lax.broadcasted_iota(jnp.int32, (groups, 128), 1)
    take = jnp.where(group % 8 == lane // CAP, 1.0, 0.0).astype(BF16)
    held = jnp.dot(spread, take, preferred_element_type=F32)
    spot = (lax.broadcasted_iota(jnp.int32, (rows, 128), 1) % CAP).astype(F32)
    return jnp.where(spot < held, keys + 1, 0)


def pack_keys(arrived, me, at):
    lane = lax.broadcasted_iota(jnp.int32, (1, 128), 1) // CAP
    mine = lax.rem(me, 8)
    for r in range(arrived.shape[0] // 8):
        line = jnp.zeros((1, 128), jnp.int32)
        for seat in range(8):
            turned = pltpu.roll(arrived[8 * r + seat], lax.rem(8 + seat - mine, 8) * CAP, 1)
            line = line + jnp.where(lane == seat, turned, 0)
        at[r:r + 1, :] = line


def dispatch_kernel(
    s_rows, s_keys, s_counts, t_rows, t_keys, t_counts, r_keys, r_counts,
    acc_s, acc_t, s_all, t_all, sk_all, tk_all, rk_all, both,
    sk_out, tk_out, rk_out, sk_in, tk_in, rk_in, lhs, rhs,
    a_send, a_recv, ring_send, ring_recv, t_send, t_recv,
    sg_send, sg_recv, tg_send, tg_recv, rg_send, rg_recv,
):
    x, core, y, z = place()
    cy = core * 4 + y
    me_s = x * 8 + cy
    me_t = z * 8 + cy
    me_r = z * 4 + x

    barrier = pltpu.get_barrier_semaphore()
    greet(barrier, 64, me_t, lambda d: dev_t(d, x))
    greet(barrier, 32, me_r, lambda d: dev_r(d, core, y))
    greet(barrier, 32, me_s, lambda d: dev_s(d, z))
    for keys, counts, out in (
        (s_keys, s_counts, sk_out), (t_keys, t_counts, tk_out), (r_keys, r_counts, rk_out)
    ):
        code = live_keys(keys[...], counts[...])
        for r in range(keys.shape[0]):
            out[r] = code[r:r + 1, :]
    acc_s[...] = jnp.zeros_like(acc_s)
    acc_t[...] = jnp.zeros_like(acc_t)
    sk_all[z] = jnp.zeros((8, 128), jnp.int32)
    rk_all[cy] = jnp.zeros((8, 128), jnp.int32)
    pl.semaphore_wait(barrier, 31 + 63 + 31)

    def send_keys(count, me, target, out, dst, n):
        pltpu.make_async_copy(out.at[lax.div(me, 8)], dst.at[me], a_recv.at[n]).start()

        def one(t, carry):
            d = lax.rem(me + t, count)
            push(out.at[lax.div(d, 8)], dst.at[me], a_send.at[n], a_recv.at[n], target(d))
            return carry

        lax.fori_loop(1, count, one, 0)

    def send_rows(count, me, target, src, dst, n):
        pltpu.make_async_copy(src.at[me], dst.at[me], a_recv.at[n]).start()

        def one(t, carry):
            d = lax.rem(me + t, count)
            push(src.at[d], dst.at[me], a_send.at[n], a_recv.at[n], target(d))
            return carry

        lax.fori_loop(1, count, one, 0)

    def to_s(d):
        return dev_s(d, z)

    def to_t(d):
        return dev_t(d, x)

    send_keys(64, me_t, to_t, tk_out, tk_in, 1)
    send_keys(32, me_s, to_s, sk_out, sk_in, 0)
    send_rows(32, me_s, to_s, s_rows, s_all.at[z], 3)
    send_rows(64, me_t, to_t, t_rows, t_all.at[x], 4)
    send_keys(32, me_r, lambda d: dev_r(d, core, y), rk_out, rk_in, 2)

    started = []
    drain(tk_in, a_recv.at[1])
    pack_keys(tk_in, me_t, tk_all.at[x])
    for o in (2, 1, 3):
        started.append(push(
            tk_all.at[x], tk_all.at[x], tg_send.at[o - 1], tg_recv.at[o - 1],
            dev(lax.rem(x + o, 4), core, y, z),
        ))
    drain(sk_in, a_recv.at[0])
    pack_keys(sk_in, me_s, sk_all.at[z])
    for o in (4, 3, 5, 2, 6, 1, 7):
        started.append(push(
            sk_all.at[z], sk_all.at[z], sg_send.at[o - 1], sg_recv.at[o - 1],
            dev(x, core, y, lax.rem(z + o, 8)),
        ))

    def ring(step, way):
        at = lax.rem(z + 8 - way * step, 8)
        lane = 0 if way == 1 else 1
        started.append(push(
            s_all.at[at], s_all.at[at], ring_send.at[lane, step], ring_recv.at[lane, step],
            dev(x, core, y, lax.rem(z + 8 + way, 8)),
        ))

    def ring_in(step, way):
        at = lax.rem(z + 8 - way * (step + 1), 8)
        drain(s_all.at[at], ring_recv.at[0 if way == 1 else 1, step])
        return at

    drain(s_all.at[z], a_recv.at[3])
    ring(0, 1)
    ring(0, -1)

    drain(rk_in, a_recv.at[2])
    pack_keys(rk_in, me_r, rk_all.at[cy])
    for o in range(1, 8):
        d = lax.rem(cy + o, 8)
        started.append(push(
            rk_all.at[cy], rk_all.at[cy], rg_send.at[o - 1], rg_recv.at[o - 1],
            dev(x, lax.div(d, 4), lax.rem(d, 4), z),
        ))
    for o in range(1, 4):
        drain(tk_all.at[lax.rem(x + 4 - o, 4)], tg_recv.at[o - 1])
    for o in range(1, 8):
        drain(sk_all.at[lax.rem(z + 8 - o, 8)], sg_recv.at[o - 1])

    def count_s(i, total):
        kv = key_line(sk_all, i, 0)
        return total + last_dims(hot(kv >> 6), hot(kv & 63))

    def count_t(i, total):
        for half in range(2):
            kv = key_line(tk_all, i, 4 * half)
            total = total + last_dims(hot(kv >> 6), hot(kv & 63))
        return total

    zero = jnp.zeros((KEYS, KEYS), F32)
    sc = lax.fori_loop(0, 8, count_s, zero)
    tc = lax.fori_loop(0, 4, count_t, zero)
    both[0] = sc
    both[1] = tc

    def low(cnt):
        return cnt - jnp.floor(cnt * (1.0 / 256.0)) * 256.0

    s_share, t_share = low(tc).astype(BF16), low(sc).astype(BF16)

    def do_s(at):
        product(
            key_line(sk_all, at, 0), s_share,
            lambda r: s_all[at, 8 * r:8 * r + 8].reshape(128, W), acc_s, lhs, rhs,
        )

    def do_t(at):
        def half(i, carry):
            kv = jnp.concatenate(
                [tk_all[at, pl.ds(4 * i + r, 1), :] for r in range(4)], axis=1
            ) - 1
            product(
                kv, t_share,
                lambda r: t_all[at, pl.ds(32 * i + 8 * r, 8)].reshape(128, W), acc_t, lhs, rhs,
            )
            return carry

        lax.fori_loop(0, 2, half, 0)

    def do_many(spots, do):
        def one(n, carry):
            at = spots[0]
            for k in range(1, len(spots)):
                at = jnp.where(n == k, spots[k], at)
            do(at)
            return carry

        lax.fori_loop(0, len(spots), one, 0)

    drain(t_all.at[x], a_recv.at[4])
    for o in (2, 1, 3):
        started.append(push(
            t_all.at[x], t_all.at[x], t_send.at[o - 1], t_recv.at[o - 1],
            dev(lax.rem(x + o, 4), core, y, z),
        ))
    behind = [z]
    for step in (0, 1, 2):
        got = [ring_in(step, 1)]
        ring(step + 1, 1)
        got.append(ring_in(step, -1))
        if step < 2:
            ring(step + 1, -1)
        do_many(behind, do_s)
        if step == 0:
            do_t(x)
        behind = got
    do_many(behind, do_s)
    do_s(ring_in(3, 1))
    spots = []
    for o in (1, 3, 2):
        at = lax.rem(x + 4 - o, 4)
        drain(t_all.at[at], t_recv.at[o - 1])
        spots.append(at)
    do_many(spots, do_t)

    for o in range(1, 8):
        drain(rk_all.at[lax.rem(cy + 8 - o, 8)], rg_recv.at[o - 1])
    for n, ref in enumerate((sk_in, tk_in, rk_in)):
        drain(ref.at[pl.ds(0, ref.shape[0] - 1)], a_send.at[n])
    for n, ref in ((3, s_rows), (4, t_rows)):
        drain(ref.at[pl.ds(0, ref.shape[0] - 1)], a_send.at[n])
    for c in started:
        c.wait_send()


def dispatch(*args):
    hbm = pl.BlockSpec(memory_space=pl.ANY)
    vm = pl.BlockSpec(memory_space=pltpu.VMEM)
    dma = pltpu.SemaphoreType.DMA
    i32 = jnp.int32
    out = (
        jax.ShapeDtypeStruct((4096, W), F32),
        jax.ShapeDtypeStruct((4096, W), F32),
        jax.ShapeDtypeStruct((8, 32, CAP, W), BF16),
        jax.ShapeDtypeStruct((4, 64, CAP, W), BF16),
        jax.ShapeDtypeStruct((8, 8, 128), i32),
        jax.ShapeDtypeStruct((4, 8, 128), i32),
        jax.ShapeDtypeStruct((8, 8, 128), i32),
        jax.ShapeDtypeStruct((2, KEYS, KEYS), F32),
    )
    return pl.pallas_call(
        dispatch_kernel,
        out_shape=out,
        in_specs=[hbm, vm, vm, hbm, vm, vm, vm, vm],
        out_specs=(vm,) * 8,
        scratch_shapes=[
            pltpu.VMEM((4, 1, 128), i32), pltpu.VMEM((8, 1, 128), i32), pltpu.VMEM((4, 1, 128), i32),
            pltpu.VMEM((32, 1, 128), i32), pltpu.VMEM((64, 1, 128), i32), pltpu.VMEM((32, 1, 128), i32),
            pltpu.VMEM((1024, CHUNK), BF16),
            pltpu.VMEM((CHUNK, 4 * W), BF16),
            dma((5,)), dma((5,)),
            dma((2, 4)), dma((2, 4)),
            dma((3,)), dma((3,)),
            dma((7,)), dma((7,)),
            dma((3,)), dma((3,)),
            dma((7,)), dma((7,)),
        ],
        compiler_params=pltpu.CompilerParams(
            collective_id=0, has_side_effects=True, vmem_limit_bytes=24 << 20
        ),
        name="dispatch",
    )(*args)


def repair_kernel(
    both, sk_all, tk_all, s_all, t_all, was_s, was_t, acc_s, acc_t, block, table, lhs, rhs, sem
):
    @pl.when(jnp.max(both[...]) >= 256.0)
    def _():
        def high(cnt):
            return (jnp.floor(cnt * (1.0 / 256.0)) * 256.0).astype(BF16)

        def move(src, dst):
            copy = pltpu.make_async_copy(src, dst, sem)
            copy.start()
            copy.wait()

        def load(r):
            return block[8 * r:8 * r + 8].reshape(128, W)

        s_share, t_share = high(both[1]), high(both[0])

        def one_s(i, carry):
            move(s_all.at[i], block)
            product(key_line(sk_all, i, 0), s_share, load, table, lhs, rhs)
            return carry

        def one_t(i, carry):
            for half in range(2):
                move(t_all.at[i, pl.ds(32 * half, 32)], block)
                product(key_line(tk_all, i, 4 * half), t_share, load, table, lhs, rhs)
            return carry

        move(was_s, table)
        lax.fori_loop(0, 8, one_s, 0)
        move(table, acc_s)
        move(was_t, table)
        lax.fori_loop(0, 4, one_t, 0)
        move(table, acc_t)


def repair(both, sk_all, tk_all, s_all, t_all, acc_s, acc_t):
    hbm = pl.BlockSpec(memory_space=pl.ANY)
    vm = pl.BlockSpec(memory_space=pltpu.VMEM)
    total = jax.ShapeDtypeStruct((4096, W), F32)
    return pl.pallas_call(
        repair_kernel,
        out_shape=(total, total),
        in_specs=[vm, vm, vm, hbm, hbm, hbm, hbm],
        out_specs=(hbm, hbm),
        input_output_aliases={5: 0, 6: 1},
        scratch_shapes=[
            pltpu.VMEM((32, CAP, W), BF16),
            pltpu.VMEM((4096, W), F32),
            pltpu.VMEM((1024, CHUNK), BF16),
            pltpu.VMEM((CHUNK, 4 * W), BF16),
            pltpu.SemaphoreType.DMA,
        ],
        compiler_params=pltpu.CompilerParams(vmem_limit_bytes=24 << 20),
        name="repair",
    )(both, sk_all, tk_all, s_all, t_all, acc_s, acc_t)


def finish_kernel(
    idx, acc_s, acc_t, rk_all, both, r_rows, out,
    away, ra, rb, h, rows, joined, sems, p_send, p_recv, y_send, y_recv,
):
    x, core, y, z = place()
    me_r = z * 4 + x
    barrier = pltpu.get_barrier_semaphore()
    pl.semaphore_signal(barrier, inc=1, device_id=dev(x, 1 - core, y, z), device_id_type=MESH)
    for o in (1, 2, 3):
        pl.semaphore_signal(
            barrier, inc=1, device_id=dev(x, core, lax.rem(y + o, 4), z), device_id_type=MESH
        )
    greet(barrier, 32, me_r, lambda d: dev_r(d, core, y))

    tri = last_dims(both[0], both[1], precision=lax.Precision.HIGHEST)
    stack = jnp.concatenate(split3(tri), axis=1)

    def gather(o, to):
        kv = jnp.concatenate([rk_all[o, r:r + 1, :] for r in range(4)], axis=1) - 1
        first = hot(kv >> 6)
        sums = jnp.dot(
            stack, jnp.concatenate([first, first, first], axis=0), preferred_element_type=F32
        )
        line = jnp.sum(sums * hot(kv & 63).astype(F32), axis=0, keepdims=True)
        for r in range(4):
            to[512 + r:513 + r, :] = line[:, 128 * r:128 * r + 128]
        to[516:520, :] = jnp.zeros((4, 128), F32)

        def some(i, carry):
            for u in range(16):
                at = idx[o * 512 + i * 16 + u]
                to[pl.ds(i * 16 + u, 1), :] = (
                    acc_s[pl.ds(at & 4095, 1), :] + acc_t[pl.ds(at >> 12, 1), :]
                )
            return carry

        lax.fori_loop(0, 32, some, 0)

    order = (2, 1, 3, 0)
    gather((1 - core) * 4 + lax.rem(y + 2, 4), away.at[2])
    pl.semaphore_wait(barrier, 1 + 3 + 31)

    pltpu.make_async_copy(r_rows.at[me_r], rows.at[me_r], sems.at[3]).start()

    def spread(t, carry):
        d = lax.rem(me_r + t, 32)
        push(r_rows.at[d], rows.at[me_r], sems.at[2], sems.at[3], dev_r(d, core, y))
        return carry

    partner, sent = [], []
    for n, o in enumerate(order):
        to = lax.rem(y + o, 4)
        if n:
            gather((1 - core) * 4 + to, away.at[o])
        partner.append(push(
            away.at[o], ra.at[o], p_send.at[o], p_recv.at[o], dev(x, 1 - core, y, z)
        ))
        if n == 0:
            lax.fori_loop(1, 32, spread, 0)
        gather(core * 4 + to, h.at[o])
        partner[n].wait_recv()
        h[o] = h[o] + ra[o]
        if o:
            sent.append(push(
                h.at[o], rb.at[o - 1], y_send.at[o - 1], y_recv.at[o - 1], dev(x, core, to, z)
            ))
    drain(rows, sems.at[3])
    for c in sent:
        c.wait_recv()
    line = h[0, 512:516, :] + rb[0, 512:516, :] + rb[1, 512:516, :] + rb[2, 512:516, :]
    scale = jnp.where(rk_all[core * 4 + y, 0:4, :] > 0, 1.0 / jnp.sqrt(1.0 + line), 0.0)
    for r in range(4):
        at = pl.ds(128 * r, 128)
        side = jnp.transpose(jnp.broadcast_to(scale[r:r + 1, :], (128, 128)))
        total = h[0, at, :] + rb[0, at, :] + rb[1, at, :] + rb[2, at, :]
        value = rows[8 * r:8 * r + 8].reshape(128, W).astype(F32) * total * side
        joined[8 * r:8 * r + 8] = value.astype(BF16).reshape(8, CAP, W)

    pltpu.make_async_copy(joined.at[me_r], out.at[me_r], sems.at[1]).start()

    def home(t, carry):
        d = lax.rem(me_r + t, 32)
        push(joined.at[d], out.at[me_r], sems.at[0], sems.at[1], dev_r(d, core, y))
        return carry

    lax.fori_loop(1, 32, home, 0)
    drain(out, sems.at[1])
    drain(joined.at[pl.ds(0, 31)], sems.at[0])
    drain(rows.at[pl.ds(0, 31)], sems.at[2])
    for c in partner + sent:
        c.wait_send()


def finish(idx, acc_s, acc_t, rk_all, both, r_rows):
    vm = pl.BlockSpec(memory_space=pltpu.VMEM)
    hbm = pl.BlockSpec(memory_space=pl.ANY)
    dma = pltpu.SemaphoreType.DMA
    return pl.pallas_call(
        finish_kernel,
        out_shape=jax.ShapeDtypeStruct((32, CAP, W), BF16),
        in_specs=[pl.BlockSpec(memory_space=pltpu.SMEM), vm, vm, vm, vm, hbm],
        out_specs=hbm,
        scratch_shapes=[
            pltpu.VMEM((4, ROWS_G, W), F32),
            pltpu.VMEM((4, ROWS_G, W), F32),
            pltpu.VMEM((3, ROWS_G, W), F32),
            pltpu.VMEM((4, ROWS_G, W), F32),
            pltpu.VMEM((32, CAP, W), BF16),
            pltpu.VMEM((32, CAP, W), BF16),
            dma((4,)), dma((4,)), dma((4,)), dma((3,)), dma((3,)),
        ],
        compiler_params=pltpu.CompilerParams(
            collective_id=1, has_side_effects=True, vmem_limit_bytes=24 << 20
        ),
        name="finish",
    )(idx, acc_s, acc_t, rk_all, both, r_rows)


def body(r_rows, r_keys, r_counts, s_rows, s_keys, s_counts, t_rows, t_keys, t_counts):
    acc_s, acc_t, s_all, t_all, sk_all, tk_all, rk_all, both = dispatch(
        s_rows.reshape(32, CAP, W), s_keys.reshape(4, 128), s_counts.reshape(1, 32),
        t_rows.reshape(64, CAP, W), t_keys.reshape(8, 128), t_counts.reshape(1, 64),
        r_keys.reshape(4, 128), r_counts.reshape(1, 32),
    )
    acc_s, acc_t = repair(both, sk_all, tk_all, s_all, t_all, acc_s, acc_t)
    kv = jnp.maximum(rk_all[:, :4] - 1, 0)
    a, b = kv >> 6, kv & 63
    at_s = (b & 3) * 1024 + (b >> 2) * 64 + a
    at_t = (a & 3) * 1024 + (a >> 2) * 64 + b
    idx = (at_s + at_t * 4096).reshape(4096)
    joined = finish(idx, acc_s, acc_t, rk_all, both, r_rows.reshape(32, CAP, W))
    return joined.reshape(512, W)


def solution(mesh):
    rows, line = P(("aa", "ba", "col"), None), P(("aa", "ba", "col"))
    return jax.shard_map(
        body, mesh=mesh, in_specs=(rows, line, line) * 3, out_specs=rows, check_vma=False
    )
```

time: 378 us -> 85.9 us (0.23)
  waiting for transfers between devices: 181 us -> 0 us
  Pallas kernels: 0 us -> 78.3 us
  starting transfers between devices: 50.3 us -> 0 us
  local copies, waits for them, and re-layouts: 51.9 us -> 7.24 us
  blocking collectives: 44 us -> 0 us
  other arithmetic: 22 us -> 0.03 us
  matrix products: 14.7 us -> 0 us
  between operations: 13.4 us -> 0.05 us
    psum x2 -> x0, waiting for transfers between devices: 84.4 us -> none  [packed_total(): total = lax.psum(jnp.concatenate([a.ravel() for a in arrays]), axis)]
    pallas_call x0 -> x3, Pallas kernels: none -> 78.3 us  [the longest x1 47.4 us: dispatch(): pl.pallas_call(dispatch_kernel, out_shape=out, in_specs=[hbm, vm, vm, hbm...]
    all_to_all x8 -> x0, starting transfers between devices: 50 us -> none  [the longest x1 9.14 us: send_second(): lax.all_to_all(counts, ('ba', 'col'), split_axis=0, concat_axis=0, tiled=...]
    reduce_scatter x1 -> x0, waiting for transfers between devices: 49.1 us -> none  [in_one_piece(): result = lax.psum_scatter(both, axis, scatter_dimension=dim, tiled=True)]
    all_to_all x8 -> x0, waiting for transfers between devices: 47 us -> none  [the longest x1 8.06 us: send_third(): lax.all_to_all(keys, ('aa', 'col'), split_axis=0, concat_axis=0, tiled=True)]
    gather x2 -> x0, local copies, waits for them, and re-layouts: 37.1 us -> none  [the longest x1 23 us: body(): rows_count = jnp.take(triangles, r_key_all, axis=0)]
    all_to_all x2 -> x0, blocking collectives: 28.1 us -> none  [the longest x1 15 us: send_home(): lax.all_to_all(joined, ('aa', 'ba'), split_axis=0, concat_axis=0, tiled=T...]
    all_gather x1 -> x0, blocking collectives: 15.9 us -> none  [body(): r_key_all = lax.all_gather(r_key_held, 'col', axis=0, tiled=True)]
  transfers between devices with their start and end apart: 11 -> 0, of which waited for: 10 -> 0; matrix products, arithmetic and copies ran while one was open for 8% -> 0% of each run, Pallas kernels for 0% -> 0%
where the time goes in v2:
time: 85.9 us; the launch traced here: 85.6 us
  Pallas kernels  78.3 us (91%)
  local copies, waits for them, and re-layouts  7.24 us (8%)
    pallas_call x1, Pallas kernels, dispatch(): pl.pallas_call(dispatch_kernel, out_shape=out, in_specs=[hbm, vm, vm, hbm...  47.4 us
    pallas_call x1, Pallas kernels, finish(): pl.pallas_call(finish_kernel, out_shape=jax.ShapeDtypeStruct((32, CAP, W)...  30.8 us
    unnamed x19, local copies, waits for them, and re-layouts  7.24 us

profile of v2, /device:TPU:1, one launch (start us, length us, event | category | flops | bytes accessed | tf_op | source)
XLA Modules:
  0.0 85.6 jit_solution(16939104697491914848)
XLA Ops:
  0.0 0.0 copy-start
  0.0 0.9 %copy-done = bf16[1024,128]{1,0:T(8,128)(2,1)S(1)} copy-done((bf16[1024,128]{1,0:T(8,128)(2,1)S(1)}, bf16[1024,128]{1,0:T(8,128)(2,1)}, u32[]{:S(2)}) %copy-start) | copy-done | bytes 262168
  1.0 0.0 copy-start.2
  1.0 0.9 %copy-done.2 = bf16[512,128]{1,0:T(8,128)(2,1)S(1)} copy-done((bf16[512,128]{1,0:T(8,128)(2,1)S(1)}, bf16[512,128]{1,0:T(8,128)(2,1)}, u32[]{:S(2)}) %copy-start.2) | copy-done | bytes 131096
  1.9 0.0 copy-start.3
  1.9 0.7 copy-done.3
  2.5 0.0 copy-start.4
  2.5 0.7 copy-done.4
  3.2 0.0 copy-start.5
  3.2 0.7 copy-done.5
  3.9 0.0 copy-start.6
  3.9 0.7 copy-done.6
  4.6 0.0 copy-start.7
  4.6 0.7 copy-done.7
  5.2 0.0 copy-start.8
  5.2 0.7 copy-done.8
  5.9 47.4 %dispatch.1 = (f32[4096,128]{1,0:T(8,128)S(1)}, f32[4096,128]{1,0:T(8,128)S(1)}, bf16[8,32,16,128]{3,2,1,0:T(8,128)(2,1)S(1)}, bf16[4,64,16,128]{3,2,1,0:T(8,128...) custom-call(bf16[32,16,128]{2,1,0:T(8,128)(2,1)S(1)} %bitcast.14, ...), custom_call_target="tpu_custom_call" | custom-call | tf_op jit(solution)/shard_map/dispatch/pallas_call | solution.py:336
  53.2 0.0 copy-start.1
  53.3 0.1 repair.1
  53.4 0.7 copy-done.1
  54.2 30.8 %finish.1 = bf16[32,16,128]{2,1,0:T(8,128)(2,1)S(1)} custom-call(s32[4096]{0:T(1024)S(1)} %bitcast.15, f32[4096,128]{1,0:T(8,128)S(1)} %get-tuple-element.23.acc_s, f32[4096,128]{1,0:T(8,128)S(1)} %get-tuple-element.24.acc_t, s32[8,8,128]{2,1,0:T(8,128)S(1)} %get-tuple-element.15.rk_all, f32[2,64,64]{2,1,0:T(8,128)S(1)} %get-tuple-element.16.both, ...), custom_call_target="tpu_custom_call" | custom-call | tf_op jit(solution)/shard_map/finish/pallas_call | solution.py:516
  85.0 0.7 copy.16
  (1 shorter events, 0.0 us)
Async XLA Ops:
  0.0 0.9 %copy-start = (bf16[1024,128]{1,0:T(8,128)(2,1)S(1)}, bf16[1024,128]{1,0:T(8,128)(2,1)}, u32[]{:S(2)}) copy-start(bf16[1024,128]{1,0:T(8,128)(2,1)} %param.15) | copy-start | bytes 786436
  1.0 0.9 %copy-start.2 = (bf16[512,128]{1,0:T(8,128)(2,1)S(1)}, bf16[512,128]{1,0:T(8,128)(2,1)}, u32[]{:S(2)}) copy-start(bf16[512,128]{1,0:T(8,128)(2,1)} %param.12) | copy-start | bytes 393220
  1.9 0.7 copy-start.3
  2.5 0.7 copy-start.4
  3.2 0.7 copy-start.5
  3.9 0.7 copy-start.6
  4.6 0.7 copy-start.7
  5.2 0.7 copy-start.8
  53.2 0.9 %copy-start.1 = (bf16[512,128]{1,0:T(8,128)(2,1)S(1)}, bf16[512,128]{1,0:T(8,128)(2,1)}, u32[]{:S(2)}) copy-start(bf16[512,128]{1,0:T(8,128)(2,1)} %param.9) | copy-start | bytes 393220

commit v3 on v2

--- a/solution.py
+++ b/solution.py
@@ -11,6 +11,7 @@
 MESH = pl.DeviceIdType.MESH
 CHUNK = 512
 ROWS_G = 520
+HALF_G = 256
 F32 = jnp.float32
 BF16 = jnp.bfloat16
 
@@ -24,26 +25,55 @@
     return (2 * x + core, y, z)
 
 
-def dev_s(d, z):
-    return dev(lax.div(d, 8), lax.rem(lax.div(d, 4), 2), lax.rem(d, 4), z)
-
-
-def dev_t(d, x):
-    return dev(x, lax.rem(lax.div(d, 4), 2), lax.rem(d, 4), lax.div(d, 8))
-
-
-def dev_r(d, core, y):
-    return dev(lax.rem(d, 4), core, y, lax.div(d, 4))
-
-
-def greet(barrier, count, me, target):
+def around(me, count):
+    return [me] + [lax.rem(me + k, count) for k in range(1, count)]
+
+
+def seats(cy):
+    return [(d, lax.div(d, 4), lax.rem(d, 4)) for d in around(cy, 8)]
+
+
+def each_s(x, cy, z, do):
+    near = seats(cy)
+    for n, xx in enumerate(around(x, 4)):
+        for m, (d, core, y) in enumerate(near):
+            if n or m:
+                do(xx * 8 + d, xx, dev(xx, core, y, z))
+
+
+def each_t(x, cy, z, do):
+    near = seats(cy)
+    for d, core, y in near[1:]:
+        do(z * 8 + d, z, dev(x, core, y, z))
+
     def one(t, carry):
-        pl.semaphore_signal(
-            barrier, inc=1, device_id=target(lax.rem(me + t, count)), device_id_type=MESH
-        )
+        zz = lax.rem(z + t, 8)
+        for d, core, y in near:
+            do(zz * 8 + d, zz, dev(x, core, y, zz))
         return carry
 
-    lax.fori_loop(1, count, one, 0)
+    lax.fori_loop(1, 8, one, 0)
+
+
+def each_r(x, core, y, z, do):
+    near = around(x, 4)
+    for xx in near[1:]:
+        do(z * 4 + xx, lax.div(z, 2), dev(xx, core, y, z))
+
+    def one(t, carry):
+        zz = lax.rem(z + t, 8)
+        for xx in near:
+            do(zz * 4 + xx, lax.div(zz, 2), dev(xx, core, y, zz))
+        return carry
+
+    lax.fori_loop(1, 8, one, 0)
+
+
+def greet(barrier):
+    def do(d, row, target):
+        pl.semaphore_signal(barrier, inc=1, device_id=target, device_id_type=MESH)
+
+    return do
 
 
 def drain(ref, sem):
@@ -128,7 +158,8 @@
 def dispatch_kernel(
     s_rows, s_keys, s_counts, t_rows, t_keys, t_counts, r_keys, r_counts,
     acc_s, acc_t, s_all, t_all, sk_all, tk_all, rk_all, both,
-    sk_out, tk_out, rk_out, sk_in, tk_in, rk_in, lhs, rhs,
+    sk_own, tk_own, rk_own, sc_own, tc_own, rc_own,
+    sk_out, tk_out, rk_out, sk_in, tk_in, rk_in, lhs, rhs, own_sems,
     a_send, a_recv, ring_send, ring_recv, t_send, t_recv,
     sg_send, sg_recv, tg_send, tg_recv, rg_send, rg_recv,
 ):
@@ -138,12 +169,23 @@
     me_t = z * 8 + cy
     me_r = z * 4 + x
 
+    fetched = [
+        pltpu.make_async_copy(src, dst, own_sems.at[n])
+        for n, (src, dst) in enumerate((
+            (t_keys, tk_own), (t_counts, tc_own), (s_keys, sk_own),
+            (s_counts, sc_own), (r_keys, rk_own), (r_counts, rc_own),
+        ))
+    ]
+    for c in fetched:
+        c.start()
     barrier = pltpu.get_barrier_semaphore()
-    greet(barrier, 64, me_t, lambda d: dev_t(d, x))
-    greet(barrier, 32, me_r, lambda d: dev_r(d, core, y))
-    greet(barrier, 32, me_s, lambda d: dev_s(d, z))
+    each_t(x, cy, z, greet(barrier))
+    each_r(x, core, y, z, greet(barrier))
+    each_s(x, cy, z, greet(barrier))
+    for c in fetched:
+        c.wait()
     for keys, counts, out in (
-        (s_keys, s_counts, sk_out), (t_keys, t_counts, tk_out), (r_keys, r_counts, rk_out)
+        (sk_own, sc_own, sk_out), (tk_own, tc_own, tk_out), (rk_own, rc_own, rk_out)
     ):
         code = live_keys(keys[...], counts[...])
         for r in range(keys.shape[0]):
@@ -154,39 +196,59 @@
     rk_all[cy] = jnp.zeros((8, 128), jnp.int32)
     pl.semaphore_wait(barrier, 31 + 63 + 31)
 
-    def send_keys(count, me, target, out, dst, n):
-        pltpu.make_async_copy(out.at[lax.div(me, 8)], dst.at[me], a_recv.at[n]).start()
-
-        def one(t, carry):
-            d = lax.rem(me + t, count)
-            push(out.at[lax.div(d, 8)], dst.at[me], a_send.at[n], a_recv.at[n], target(d))
-            return carry
-
-        lax.fori_loop(1, count, one, 0)
-
-    def send_rows(count, me, target, src, dst, n):
-        pltpu.make_async_copy(src.at[me], dst.at[me], a_recv.at[n]).start()
-
-        def one(t, carry):
-            d = lax.rem(me + t, count)
-            push(src.at[d], dst.at[me], a_send.at[n], a_recv.at[n], target(d))
-            return carry
-
-        lax.fori_loop(1, count, one, 0)
-
-    def to_s(d):
-        return dev_s(d, z)
-
-    def to_t(d):
-        return dev_t(d, x)
-
-    send_keys(64, me_t, to_t, tk_out, tk_in, 1)
-    send_keys(32, me_s, to_s, sk_out, sk_in, 0)
-    send_rows(32, me_s, to_s, s_rows, s_all.at[z], 3)
-    send_rows(64, me_t, to_t, t_rows, t_all.at[x], 4)
-    send_keys(32, me_r, lambda d: dev_r(d, core, y), rk_out, rk_in, 2)
+    def keys_to(out, dst, me, n):
+        def do(d, row, target):
+            push(out.at[row], dst.at[me], a_send.at[n], a_recv.at[n], target)
+
+        return do
+
+    def rows_to(src, dst, me, n):
+        def do(d, row, target):
+            push(src.at[d], dst.at[me], a_send.at[n], a_recv.at[n], target)
+
+        return do
+
+    each_t(x, cy, z, keys_to(tk_out, tk_in, me_t, 1))
+    each_s(x, cy, z, keys_to(sk_out, sk_in, me_s, 0))
+    each_s(x, cy, z, rows_to(s_rows, s_all.at[z], me_s, 3))
+    each_t(x, cy, z, rows_to(t_rows, t_all.at[x], me_t, 4))
+    for n, src, dst in (
+        (0, sk_out.at[x], sk_in.at[me_s]),
+        (1, tk_out.at[z], tk_in.at[me_t]),
+        (2, rk_out.at[lax.div(z, 2)], rk_in.at[me_r]),
+        (3, s_rows.at[me_s], s_all.at[z, me_s]),
+        (4, t_rows.at[me_t], t_all.at[x, me_t]),
+    ):
+        pltpu.make_async_copy(src, dst, a_recv.at[n]).start()
+    each_r(x, core, y, z, keys_to(rk_out, rk_in, me_r, 2))
 
     started = []
+
+    def ring(step, way):
+        at = lax.rem(z + 8 - way * step, 8)
+        lane = 0 if way == 1 else 1
+        started.append(push(
+            s_all.at[at], s_all.at[at], ring_send.at[lane, step], ring_recv.at[lane, step],
+            dev(x, core, y, lax.rem(z + 8 + way, 8)),
+        ))
+
+    def ring_in(step, way):
+        at = lax.rem(z + 8 - way * (step + 1), 8)
+        drain(s_all.at[at], ring_recv.at[0 if way == 1 else 1, step])
+        return at
+
+    def x_half(block, half, way, n):
+        part = t_all.at[block, pl.ds(32 * half, 32)]
+        started.append(push(
+            part, part, t_send.at[n], t_recv.at[n], dev(lax.rem(x + 4 + way, 4), core, y, z)
+        ))
+
+    def x_in(block, half, n):
+        drain(t_all.at[block, pl.ds(32 * half, 32)], t_recv.at[n])
+
+    drain(s_all.at[z], a_recv.at[3])
+    ring(0, 1)
+    ring(0, -1)
     drain(tk_in, a_recv.at[1])
     pack_keys(tk_in, me_t, tk_all.at[x])
     for o in (2, 1, 3):
@@ -201,23 +263,15 @@
             sk_all.at[z], sk_all.at[z], sg_send.at[o - 1], sg_recv.at[o - 1],
             dev(x, core, y, lax.rem(z + o, 8)),
         ))
-
-    def ring(step, way):
-        at = lax.rem(z + 8 - way * step, 8)
-        lane = 0 if way == 1 else 1
-        started.append(push(
-            s_all.at[at], s_all.at[at], ring_send.at[lane, step], ring_recv.at[lane, step],
-            dev(x, core, y, lax.rem(z + 8 + way, 8)),
-        ))
-
-    def ring_in(step, way):
-        at = lax.rem(z + 8 - way * (step + 1), 8)
-        drain(s_all.at[at], ring_recv.at[0 if way == 1 else 1, step])
-        return at
-
-    drain(s_all.at[z], a_recv.at[3])
-    ring(0, 1)
-    ring(0, -1)
+    drain(t_all.at[x], a_recv.at[4])
+    x_half(x, 0, 1, 0)
+    x_half(x, 1, -1, 1)
+    x_half(x, 1, 1, 2)
+    x_half(x, 0, -1, 3)
+    got = [ring_in(0, 1)]
+    ring(1, 1)
+    got.append(ring_in(0, -1))
+    ring(1, -1)
 
     drain(rk_in, a_recv.at[2])
     pack_keys(rk_in, me_r, rk_all.at[cy])
@@ -282,31 +336,30 @@
 
         lax.fori_loop(0, len(spots), one, 0)
 
-    drain(t_all.at[x], a_recv.at[4])
-    for o in (2, 1, 3):
-        started.append(push(
-            t_all.at[x], t_all.at[x], t_send.at[o - 1], t_recv.at[o - 1],
-            dev(lax.rem(x + o, 4), core, y, z),
-        ))
-    behind = [z]
-    for step in (0, 1, 2):
-        got = [ring_in(step, 1)]
-        ring(step + 1, 1)
-        got.append(ring_in(step, -1))
-        if step < 2:
-            ring(step + 1, -1)
-        do_many(behind, do_s)
-        if step == 0:
-            do_t(x)
-        behind = got
-    do_many(behind, do_s)
-    do_s(ring_in(3, 1))
-    spots = []
-    for o in (1, 3, 2):
-        at = lax.rem(x + 4 - o, 4)
-        drain(t_all.at[at], t_recv.at[o - 1])
-        spots.append(at)
-    do_many(spots, do_t)
+    before, after, far = lax.rem(x + 3, 4), lax.rem(x + 1, 4), lax.rem(x + 2, 4)
+    do_t(x)
+    x_in(before, 0, 0)
+    x_half(before, 0, 1, 4)
+    x_in(after, 1, 1)
+    x_half(after, 1, -1, 5)
+    do_s(z)
+    later = [ring_in(1, 1)]
+    ring(2, 1)
+    later.append(ring_in(1, -1))
+    ring(2, -1)
+    do_many(got, do_s)
+    got = [ring_in(2, 1)]
+    ring(3, 1)
+    x_in(before, 1, 2)
+    x_in(after, 0, 3)
+    do_many(later, do_s)
+    do_many([before, after], do_t)
+    got.append(ring_in(2, -1))
+    got.append(ring_in(3, 1))
+    do_many(got, do_s)
+    x_in(far, 0, 4)
+    x_in(far, 1, 5)
+    do_t(far)
 
     for o in range(1, 8):
         drain(rk_all.at[lax.rem(cy + 8 - o, 8)], rg_recv.at[o - 1])
@@ -319,7 +372,6 @@
 
 
 def dispatch(*args):
-    hbm = pl.BlockSpec(memory_space=pl.ANY)
     vm = pl.BlockSpec(memory_space=pltpu.VMEM)
     dma = pltpu.SemaphoreType.DMA
     i32 = jnp.int32
@@ -336,16 +388,19 @@
     return pl.pallas_call(
         dispatch_kernel,
         out_shape=out,
-        in_specs=[hbm, vm, vm, hbm, vm, vm, vm, vm],
+        in_specs=[pl.BlockSpec(memory_space=pltpu.HBM)] * 8,
         out_specs=(vm,) * 8,
         scratch_shapes=[
+            pltpu.VMEM((4, 128), i32), pltpu.VMEM((8, 128), i32), pltpu.VMEM((4, 128), i32),
+            pltpu.VMEM((1, 32), i32), pltpu.VMEM((1, 64), i32), pltpu.VMEM((1, 32), i32),
             pltpu.VMEM((4, 1, 128), i32), pltpu.VMEM((8, 1, 128), i32), pltpu.VMEM((4, 1, 128), i32),
             pltpu.VMEM((32, 1, 128), i32), pltpu.VMEM((64, 1, 128), i32), pltpu.VMEM((32, 1, 128), i32),
             pltpu.VMEM((1024, CHUNK), BF16),
             pltpu.VMEM((CHUNK, 4 * W), BF16),
+            dma((6,)),
             dma((5,)), dma((5,)),
             dma((2, 4)), dma((2, 4)),
-            dma((3,)), dma((3,)),
+            dma((6,)), dma((6,)),
             dma((7,)), dma((7,)),
             dma((3,)), dma((3,)),
             dma((7,)), dma((7,)),
@@ -354,7 +409,7 @@
             collective_id=0, has_side_effects=True, vmem_limit_bytes=24 << 20
         ),
         name="dispatch",
-    )(*args)
+    )(*(pltpu.with_memory_space_constraint(a, pltpu.HBM) for a in args))
 
 
 def repair_kernel(
@@ -428,7 +483,7 @@
         pl.semaphore_signal(
             barrier, inc=1, device_id=dev(x, core, lax.rem(y + o, 4), z), device_id_type=MESH
         )
-    greet(barrier, 32, me_r, lambda d: dev_r(d, core, y))
+    each_r(x, core, y, z, greet(barrier))
 
     tri = last_dims(both[0], both[1], precision=lax.Precision.HIGHEST)
     stack = jnp.concatenate(split3(tri), axis=1)
@@ -454,64 +509,83 @@
 
         lax.fori_loop(0, 32, some, 0)
 
-    order = (2, 1, 3, 0)
-    gather((1 - core) * 4 + lax.rem(y + 2, 4), away.at[2])
+    up, down = dev(x, core, lax.rem(y + 1, 4), z), dev(x, core, lax.rem(y + 3, 4), z)
+    top, low = pl.ds(0, HALF_G), pl.ds(HALF_G, ROWS_G - HALF_G)
+
+    def theirs(o):
+        return (1 - core) * 4 + lax.rem(y + o, 4)
+
+    def spread(d, row, target):
+        push(r_rows.at[d], rows.at[me_r], sems.at[2], sems.at[3], target)
+
+    partner, sent = {}, []
+
+    def to_partner(o):
+        partner[o] = push(
+            away.at[o], ra.at[o], p_send.at[o], p_recv.at[o], dev(x, 1 - core, y, z)
+        )
+
+    def meet(o):
+        gather(core * 4 + lax.rem(y + o, 4), h.at[o])
+        partner[o].wait_recv()
+        h[o] = h[o] + ra[o]
+
+    def to_y(src, dst, n, target):
+        sent.append(push(src, dst, y_send.at[n], y_recv.at[n], target))
+
+    gather(theirs(2), away.at[2])
     pl.semaphore_wait(barrier, 1 + 3 + 31)
-
+    to_partner(2)
+    gather(theirs(1), away.at[1])
+    to_partner(1)
+    meet(2)
+    to_y(h.at[2, top], rb.at[2, top], 0, up)
+    to_y(h.at[2, low], rb.at[2, low], 1, down)
+    gather(theirs(3), away.at[3])
+    to_partner(3)
+    meet(1)
+    to_y(h.at[1, low], rb.at[0, low], 2, up)
+    gather(theirs(0), away.at[0])
+    to_partner(0)
+    meet(3)
+    to_y(h.at[3, top], rb.at[1, top], 3, down)
+    drain(rb.at[2, top], y_recv.at[0])
+    h[1, top, :] = h[1, top, :] + rb[2, top, :]
+    to_y(h.at[1, top], rb.at[0, top], 4, up)
+    drain(rb.at[2, low], y_recv.at[1])
+    h[3, low, :] = h[3, low, :] + rb[2, low, :]
+    to_y(h.at[3, low], rb.at[1, low], 5, down)
     pltpu.make_async_copy(r_rows.at[me_r], rows.at[me_r], sems.at[3]).start()
-
-    def spread(t, carry):
-        d = lax.rem(me_r + t, 32)
-        push(r_rows.at[d], rows.at[me_r], sems.at[2], sems.at[3], dev_r(d, core, y))
-        return carry
-
-    partner, sent = [], []
-    for n, o in enumerate(order):
-        to = lax.rem(y + o, 4)
-        if n:
-            gather((1 - core) * 4 + to, away.at[o])
-        partner.append(push(
-            away.at[o], ra.at[o], p_send.at[o], p_recv.at[o], dev(x, 1 - core, y, z)
-        ))
-        if n == 0:
-            lax.fori_loop(1, 32, spread, 0)
-        gather(core * 4 + to, h.at[o])
-        partner[n].wait_recv()
-        h[o] = h[o] + ra[o]
-        if o:
-            sent.append(push(
-                h.at[o], rb.at[o - 1], y_send.at[o - 1], y_recv.at[o - 1], dev(x, core, to, z)
-            ))
+    each_r(x, core, y, z, spread)
+    meet(0)
     drain(rows, sems.at[3])
-    for c in sent:
-        c.wait_recv()
-    line = h[0, 512:516, :] + rb[0, 512:516, :] + rb[1, 512:516, :] + rb[2, 512:516, :]
+    for n, part in ((2, rb.at[0, low]), (3, rb.at[1, top]), (4, rb.at[0, top]), (5, rb.at[1, low])):
+        drain(part, y_recv.at[n])
+    line = h[0, 512:516, :] + rb[0, 512:516, :] + rb[1, 512:516, :]
     scale = jnp.where(rk_all[core * 4 + y, 0:4, :] > 0, 1.0 / jnp.sqrt(1.0 + line), 0.0)
     for r in range(4):
         at = pl.ds(128 * r, 128)
         side = jnp.transpose(jnp.broadcast_to(scale[r:r + 1, :], (128, 128)))
-        total = h[0, at, :] + rb[0, at, :] + rb[1, at, :] + rb[2, at, :]
+        total = h[0, at, :] + rb[0, at, :] + rb[1, at, :]
         value = rows[8 * r:8 * r + 8].reshape(128, W).astype(F32) * total * side
         joined[8 * r:8 * r + 8] = value.astype(BF16).reshape(8, CAP, W)
 
     pltpu.make_async_copy(joined.at[me_r], out.at[me_r], sems.at[1]).start()
 
-    def home(t, carry):
-        d = lax.rem(me_r + t, 32)
-        push(joined.at[d], out.at[me_r], sems.at[0], sems.at[1], dev_r(d, core, y))
-        return carry
-
-    lax.fori_loop(1, 32, home, 0)
+    def home(d, row, target):
+        push(joined.at[d], out.at[me_r], sems.at[0], sems.at[1], target)
+
+    each_r(x, core, y, z, home)
     drain(out, sems.at[1])
     drain(joined.at[pl.ds(0, 31)], sems.at[0])
     drain(rows.at[pl.ds(0, 31)], sems.at[2])
-    for c in partner + sent:
+    for c in list(partner.values()) + sent:
         c.wait_send()
 
 
 def finish(idx, acc_s, acc_t, rk_all, both, r_rows):
     vm = pl.BlockSpec(memory_space=pltpu.VMEM)
-    hbm = pl.BlockSpec(memory_space=pl.ANY)
+    hbm = pl.BlockSpec(memory_space=pltpu.HBM)
     dma = pltpu.SemaphoreType.DMA
     return pl.pallas_call(
         finish_kernel,
@@ -525,13 +599,13 @@
             pltpu.VMEM((4, ROWS_G, W), F32),
             pltpu.VMEM((32, CAP, W), BF16),
             pltpu.VMEM((32, CAP, W), BF16),
-            dma((4,)), dma((4,)), dma((4,)), dma((3,)), dma((3,)),
+            dma((4,)), dma((4,)), dma((4,)), dma((6,)), dma((6,)),
         ],
         compiler_params=pltpu.CompilerParams(
             collective_id=1, has_side_effects=True, vmem_limit_bytes=24 << 20
         ),
         name="finish",
-    )(idx, acc_s, acc_t, rk_all, both, r_rows)
+    )(idx, acc_s, acc_t, rk_all, both, pltpu.with_memory_space_constraint(r_rows, pltpu.HBM))
 
 
 def body(r_rows, r_keys, r_counts, s_rows, s_keys, s_counts, t_rows, t_keys, t_counts):

time: 85.9 us -> 71.9 us (0.84); the launches traced: 85.6 us -> 70.6 us
  Pallas kernels: 78.3 us -> 69.9 us
  local copies, waits for them, and re-layouts: 7.24 us -> 0.66 us
    unnamed x19 -> x1, local copies, waits for them, and re-layouts: 7.24 us -> 0.66 us
    pallas_call x1, Pallas kernels: 30.8 us -> 25.7 us  [finish(): pl.pallas_call(finish_kernel, out_shape=jax.ShapeDtypeStruct((32, CAP, W)...]
    pallas_call x1, Pallas kernels: 47.4 us -> 44 us  [dispatch(): pl.pallas_call(dispatch_kernel, out_shape=out, in_specs=[pl.BlockSpec(mem...]
where the time goes in v3:
time: 71.9 us; the launch traced here: 70.6 us
  Pallas kernels  69.9 us (97%)
    pallas_call x1, Pallas kernels, dispatch(): pl.pallas_call(dispatch_kernel, out_shape=out, in_specs=[pl.BlockSpec(mem...  44 us
    pallas_call x1, Pallas kernels, finish(): pl.pallas_call(finish_kernel, out_shape=jax.ShapeDtypeStruct((32, CAP, W)...  25.7 us

profile of v3, /device:TPU:1, one launch (start us, length us, event | category | flops | bytes accessed | tf_op | source)
XLA Modules:
  0.0 70.6 jit_solution(16254500345522250608)
XLA Ops:
  0.0 44.0 %dispatch.1 = (f32[4096,128]{1,0:T(8,128)S(1)}, f32[4096,128]{1,0:T(8,128)S(1)}, bf16[8,32,16,128]{3,2,1,0:T(8,128)(2,1)S(1)}, bf16[4,64,16,128]{3,2,1,0:T(8,128...) custom-call(bf16[32,16,128]{2,1,0:T(8,128)(2,1)} %bitcast.15, ...), custom_call_target="tpu_custom_call" | custom-call | tf_op jit(solution)/shard_map/dispatch/pallas_call | solution.py:388
  44.0 0.1 repair.1
  44.2 25.7 %finish.1 = bf16[32,16,128]{2,1,0:T(8,128)(2,1)S(1)} custom-call(s32[4096]{0:T(1024)S(1)} %bitcast.12, f32[4096,128]{1,0:T(8,128)S(1)} %get-tuple-element.23.acc_s, f32[4096,128]{1,0:T(8,128)S(1)} %get-tuple-element.24.acc_t, s32[8,8,128]{2,1,0:T(8,128)S(1)} %get-tuple-element.15.rk_all, f32[2,64,64]{2,1,0:T(8,128)S(1)} %get-tuple-element.16.both, ...), custom_call_target="tpu_custom_call" | custom-call | tf_op jit(solution)/shard_map/finish/pallas_call | solution.py:590
  70.0 0.7 copy.16
  (1 shorter events, 0.0 us)

commit v4 on v3

--- a/solution.py
+++ b/solution.py
@@ -90,7 +90,7 @@
 
 
 def hot(values):
-    rows = lax.broadcasted_iota(jnp.int32, (KEYS, CHUNK), 0)
+    rows = lax.broadcasted_iota(jnp.int32, (KEYS, values.shape[1]), 0)
     return jnp.where(rows == values, 1.0, 0.0).astype(BF16)
 
 
@@ -117,7 +117,7 @@
     for h in range(16):
         mask = jnp.where(outer == h, 1.0, 0.0)
         lhs[64 * h:64 * h + 64, :] = (seen * mask).astype(BF16)
-    for r in range(4):
+    for r in range(kv.shape[1] // 128):
         side = jnp.transpose(jnp.broadcast_to(inner[:, 128 * r:128 * r + 128], (128, 128)))
         block = load(r).astype(F32)
         for q in range(4):
@@ -220,21 +220,28 @@
         (4, t_rows.at[me_t], t_all.at[x, me_t]),
     ):
         pltpu.make_async_copy(src, dst, a_recv.at[n]).start()
+
     each_r(x, core, y, z, keys_to(rk_out, rk_in, me_r, 2))
 
     started = []
 
-    def ring(step, way):
-        at = lax.rem(z + 8 - way * step, 8)
+    def ring(step, way, half):
+        at = s_all.at[lax.rem(z + 8 - way * step, 8), pl.ds(16 * half, 16)]
         lane = 0 if way == 1 else 1
         started.append(push(
-            s_all.at[at], s_all.at[at], ring_send.at[lane, step], ring_recv.at[lane, step],
+            at, at, ring_send.at[lane, step, half], ring_recv.at[lane, step, half],
             dev(x, core, y, lax.rem(z + 8 + way, 8)),
         ))
 
-    def ring_in(step, way):
+    def relay(step, way, last=False):
         at = lax.rem(z + 8 - way * (step + 1), 8)
-        drain(s_all.at[at], ring_recv.at[0 if way == 1 else 1, step])
+        for half in range(2):
+            drain(
+                s_all.at[at, pl.ds(16 * half, 16)],
+                ring_recv.at[0 if way == 1 else 1, step, half],
+            )
+            if not last:
+                ring(step + 1, way, half)
         return at
 
     def x_half(block, half, way, n):
@@ -247,8 +254,9 @@
         drain(t_all.at[block, pl.ds(32 * half, 32)], t_recv.at[n])
 
     drain(s_all.at[z], a_recv.at[3])
-    ring(0, 1)
-    ring(0, -1)
+    for half in range(2):
+        ring(0, 1, half)
+        ring(0, -1, half)
     drain(tk_in, a_recv.at[1])
     pack_keys(tk_in, me_t, tk_all.at[x])
     for o in (2, 1, 3):
@@ -263,16 +271,12 @@
             sk_all.at[z], sk_all.at[z], sg_send.at[o - 1], sg_recv.at[o - 1],
             dev(x, core, y, lax.rem(z + o, 8)),
         ))
+    one, two = relay(0, 1), relay(0, -1)
     drain(t_all.at[x], a_recv.at[4])
     x_half(x, 0, 1, 0)
     x_half(x, 1, -1, 1)
     x_half(x, 1, 1, 2)
     x_half(x, 0, -1, 3)
-    got = [ring_in(0, 1)]
-    ring(1, 1)
-    got.append(ring_in(0, -1))
-    ring(1, -1)
-
     drain(rk_in, a_recv.at[2])
     pack_keys(rk_in, me_r, rk_all.at[cy])
     for o in range(1, 8):
@@ -307,56 +311,37 @@
 
     s_share, t_share = low(tc).astype(BF16), low(sc).astype(BF16)
 
-    def do_s(at):
+    def do_s(first, second):
+        spots = (first, second)
+        kv = jnp.concatenate([key_line(sk_all, at, 0) for at in spots], axis=1)
         product(
-            key_line(sk_all, at, 0), s_share,
-            lambda r: s_all[at, 8 * r:8 * r + 8].reshape(128, W), acc_s, lhs, rhs,
+            kv, s_share,
+            lambda r: s_all[spots[r // 4], 8 * (r % 4):8 * (r % 4) + 8].reshape(128, W),
+            acc_s, lhs, rhs,
         )
 
     def do_t(at):
-        def half(i, carry):
-            kv = jnp.concatenate(
-                [tk_all[at, pl.ds(4 * i + r, 1), :] for r in range(4)], axis=1
-            ) - 1
-            product(
-                kv, t_share,
-                lambda r: t_all[at, pl.ds(32 * i + 8 * r, 8)].reshape(128, W), acc_t, lhs, rhs,
-            )
-            return carry
-
-        lax.fori_loop(0, 2, half, 0)
-
-    def do_many(spots, do):
-        def one(n, carry):
-            at = spots[0]
-            for k in range(1, len(spots)):
-                at = jnp.where(n == k, spots[k], at)
-            do(at)
-            return carry
-
-        lax.fori_loop(0, len(spots), one, 0)
-
+        kv = jnp.concatenate([key_line(tk_all, at, 0), key_line(tk_all, at, 4)], axis=1)
+        product(
+            kv, t_share, lambda r: t_all[at, 8 * r:8 * r + 8].reshape(128, W), acc_t, lhs, rhs
+        )
+
+    do_s(z, one)
+    three, four = relay(1, 1), relay(1, -1)
+    do_s(two, three)
+    do_t(x)
     before, after, far = lax.rem(x + 3, 4), lax.rem(x + 1, 4), lax.rem(x + 2, 4)
-    do_t(x)
     x_in(before, 0, 0)
     x_half(before, 0, 1, 4)
     x_in(after, 1, 1)
     x_half(after, 1, -1, 5)
-    do_s(z)
-    later = [ring_in(1, 1)]
-    ring(2, 1)
-    later.append(ring_in(1, -1))
-    ring(2, -1)
-    do_many(got, do_s)
-    got = [ring_in(2, 1)]
-    ring(3, 1)
+    five, six = relay(2, 1), relay(2, -1, True)
+    do_s(four, five)
     x_in(before, 1, 2)
+    do_t(before)
     x_in(after, 0, 3)
-    do_many(later, do_s)
-    do_many([before, after], do_t)
-    got.append(ring_in(2, -1))
-    got.append(ring_in(3, 1))
-    do_many(got, do_s)
+    do_t(after)
+    do_s(six, relay(3, 1, True))
     x_in(far, 0, 4)
     x_in(far, 1, 5)
     do_t(far)
@@ -395,11 +380,11 @@
             pltpu.VMEM((1, 32), i32), pltpu.VMEM((1, 64), i32), pltpu.VMEM((1, 32), i32),
             pltpu.VMEM((4, 1, 128), i32), pltpu.VMEM((8, 1, 128), i32), pltpu.VMEM((4, 1, 128), i32),
             pltpu.VMEM((32, 1, 128), i32), pltpu.VMEM((64, 1, 128), i32), pltpu.VMEM((32, 1, 128), i32),
-            pltpu.VMEM((1024, CHUNK), BF16),
-            pltpu.VMEM((CHUNK, 4 * W), BF16),
+            pltpu.VMEM((1024, 2 * CHUNK), BF16),
+            pltpu.VMEM((2 * CHUNK, 4 * W), BF16),
             dma((6,)),
             dma((5,)), dma((5,)),
-            dma((2, 4)), dma((2, 4)),
+            dma((2, 4, 2)), dma((2, 4, 2)),
             dma((6,)), dma((6,)),
             dma((7,)), dma((7,)),
             dma((3,)), dma((3,)),
@@ -473,7 +458,7 @@
 
 def finish_kernel(
     idx, acc_s, acc_t, rk_all, both, r_rows, out,
-    away, ra, rb, h, rows, joined, sems, p_send, p_recv, y_send, y_recv,
+    away, ra, rb, h, scales, rows, joined, sems, p_send, p_recv, y_send, y_recv,
 ):
     x, core, y, z = place()
     me_r = z * 4 + x
@@ -488,7 +473,7 @@
     tri = last_dims(both[0], both[1], precision=lax.Precision.HIGHEST)
     stack = jnp.concatenate(split3(tri), axis=1)
 
-    def gather(o, to):
+    def lines(o, to):
         kv = jnp.concatenate([rk_all[o, r:r + 1, :] for r in range(4)], axis=1) - 1
         first = hot(kv >> 6)
         sums = jnp.dot(
@@ -499,6 +484,7 @@
             to[512 + r:513 + r, :] = line[:, 128 * r:128 * r + 128]
         to[516:520, :] = jnp.zeros((4, 128), F32)
 
+    def gather(o, to):
         def some(i, carry):
             for u in range(16):
                 at = idx[o * 512 + i * 16 + u]
@@ -515,6 +501,9 @@
     def theirs(o):
         return (1 - core) * 4 + lax.rem(y + o, 4)
 
+    def mine(o):
+        return core * 4 + lax.rem(y + o, 4)
+
     def spread(d, row, target):
         push(r_rows.at[d], rows.at[me_r], sems.at[2], sems.at[3], target)
 
@@ -526,29 +515,37 @@
         )
 
     def meet(o):
-        gather(core * 4 + lax.rem(y + o, 4), h.at[o])
         partner[o].wait_recv()
         h[o] = h[o] + ra[o]
 
     def to_y(src, dst, n, target):
         sent.append(push(src, dst, y_send.at[n], y_recv.at[n], target))
 
+    def both_lines(o, carry):
+        lines(theirs(o), away.at[o])
+        lines(mine(o), h.at[o])
+        return carry
+
     gather(theirs(2), away.at[2])
+    lax.fori_loop(0, 4, both_lines, 0)
+    gather(mine(2), h.at[2])
+    gather(theirs(1), away.at[1])
     pl.semaphore_wait(barrier, 1 + 3 + 31)
     to_partner(2)
-    gather(theirs(1), away.at[1])
     to_partner(1)
+    gather(theirs(3), away.at[3])
+    to_partner(3)
     meet(2)
     to_y(h.at[2, top], rb.at[2, top], 0, up)
     to_y(h.at[2, low], rb.at[2, low], 1, down)
-    gather(theirs(3), away.at[3])
-    to_partner(3)
+    gather(mine(1), h.at[1])
     meet(1)
     to_y(h.at[1, low], rb.at[0, low], 2, up)
+    gather(mine(3), h.at[3])
+    meet(3)
+    to_y(h.at[3, top], rb.at[1, top], 3, down)
     gather(theirs(0), away.at[0])
     to_partner(0)
-    meet(3)
-    to_y(h.at[3, top], rb.at[1, top], 3, down)
     drain(rb.at[2, top], y_recv.at[0])
     h[1, top, :] = h[1, top, :] + rb[2, top, :]
     to_y(h.at[1, top], rb.at[0, top], 4, up)
@@ -557,25 +554,33 @@
     to_y(h.at[3, low], rb.at[1, low], 5, down)
     pltpu.make_async_copy(r_rows.at[me_r], rows.at[me_r], sems.at[3]).start()
     each_r(x, core, y, z, spread)
+    gather(mine(0), h.at[0])
     meet(0)
     drain(rows, sems.at[3])
     for n, part in ((2, rb.at[0, low]), (3, rb.at[1, top]), (4, rb.at[0, top]), (5, rb.at[1, low])):
         drain(part, y_recv.at[n])
     line = h[0, 512:516, :] + rb[0, 512:516, :] + rb[1, 512:516, :]
     scale = jnp.where(rk_all[core * 4 + y, 0:4, :] > 0, 1.0 / jnp.sqrt(1.0 + line), 0.0)
-    for r in range(4):
-        at = pl.ds(128 * r, 128)
-        side = jnp.transpose(jnp.broadcast_to(scale[r:r + 1, :], (128, 128)))
+    scales[...] = scale
+    pair = lax.div(z, 2)
+    xs = around(x, 4)
+    for k in (2, 1, 3, 0):
+        r = lax.rem(pair + k, 4)
+        at = pl.ds(pl.multiple_of(128 * r, 128), 128)
+        spot = pl.ds(8 * r, 8)
+        side = jnp.transpose(jnp.broadcast_to(scales[pl.ds(r, 1), :], (128, 128)))
         total = h[0, at, :] + rb[0, at, :] + rb[1, at, :]
-        value = rows[8 * r:8 * r + 8].reshape(128, W).astype(F32) * total * side
-        joined[8 * r:8 * r + 8] = value.astype(BF16).reshape(8, CAP, W)
-
-    pltpu.make_async_copy(joined.at[me_r], out.at[me_r], sems.at[1]).start()
-
-    def home(d, row, target):
-        push(joined.at[d], out.at[me_r], sems.at[0], sems.at[1], target)
-
-    each_r(x, core, y, z, home)
+        value = rows[spot].reshape(128, W).astype(F32) * total * side
+        joined[spot] = value.astype(BF16).reshape(8, CAP, W)
+        for zz in (4 * r + 1 - z, z) if k == 0 else (2 * r, 2 * r + 1):
+            for n, xx in enumerate(xs):
+                d = zz * 4 + xx
+                if k == 0 and zz is z and n == 0:
+                    pltpu.make_async_copy(joined.at[d], out.at[me_r], sems.at[1]).start()
+                else:
+                    push(
+                        joined.at[d], out.at[me_r], sems.at[0], sems.at[1], dev(xx, core, y, zz)
+                    )
     drain(out, sems.at[1])
     drain(joined.at[pl.ds(0, 31)], sems.at[0])
     drain(rows.at[pl.ds(0, 31)], sems.at[2])
@@ -597,6 +602,7 @@
             pltpu.VMEM((4, ROWS_G, W), F32),
             pltpu.VMEM((3, ROWS_G, W), F32),
             pltpu.VMEM((4, ROWS_G, W), F32),
+            pltpu.VMEM((4, 128), F32),
             pltpu.VMEM((32, CAP, W), BF16),
             pltpu.VMEM((32, CAP, W), BF16),
             dma((4,)), dma((4,)), dma((4,)), dma((6,)), dma((6,)),

time: 71.9 us -> 68.6 us (0.954)
  Pallas kernels: 69.9 us -> 66.8 us
    pallas_call x1, Pallas kernels: 44 us -> 40.2 us  [dispatch(): pl.pallas_call(dispatch_kernel, out_shape=out, in_specs=[pl.BlockSpec(mem...]
where the time goes in v4:
time: 68.6 us; the launch traced here: 67.5 us
  Pallas kernels  66.8 us (97%)
    pallas_call x1, Pallas kernels, dispatch(): pl.pallas_call(dispatch_kernel, out_shape=out, in_specs=[pl.BlockSpec(mem...  40.2 us
    pallas_call x1, Pallas kernels, finish(): pl.pallas_call(finish_kernel, out_shape=jax.ShapeDtypeStruct((32, CAP, W)...  26.2 us

profile of v4, /device:TPU:1, one launch (start us, length us, event | category | flops | bytes accessed | tf_op | source)
XLA Modules:
  0.0 67.5 jit_solution(1588803647262835464)
XLA Ops:
  0.0 40.2 %dispatch.1 = (f32[4096,128]{1,0:T(8,128)S(1)}, f32[4096,128]{1,0:T(8,128)S(1)}, bf16[8,32,16,128]{3,2,1,0:T(8,128)(2,1)S(1)}, bf16[4,64,16,128]{3,2,1,0:T(8,128...) custom-call(bf16[32,16,128]{2,1,0:T(8,128)(2,1)} %bitcast.15, ...), custom_call_target="tpu_custom_call" | custom-call | tf_op jit(solution)/shard_map/dispatch/pallas_call | solution.py:373
  40.3 0.3 repair.1
  40.6 26.2 %finish.1 = bf16[32,16,128]{2,1,0:T(8,128)(2,1)S(1)} custom-call(s32[4096]{0:T(1024)S(1)} %bitcast.12, f32[4096,128]{1,0:T(8,128)S(1)} %get-tuple-element.23.acc_s, f32[4096,128]{1,0:T(8,128)S(1)} %get-tuple-element.24.acc_t, s32[8,8,128]{2,1,0:T(8,128)S(1)} %get-tuple-element.15.rk_all, f32[2,64,64]{2,1,0:T(8,128)S(1)} %get-tuple-element.16.both, ...), custom_call_target="tpu_custom_call" | custom-call | tf_op jit(solution)/shard_map/finish/pallas_call | solution.py:595
  66.8 0.7 copy.16
  (1 shorter events, 0.0 us)

commit v5 on v4

--- a/solution.py
+++ b/solution.py
@@ -457,7 +457,7 @@
 
 
 def finish_kernel(
-    idx, acc_s, acc_t, rk_all, both, r_rows, out,
+    at_s, at_t, acc_s, acc_t, rk_all, both, r_rows, out,
     away, ra, rb, h, scales, rows, joined, sems, p_send, p_recv, y_send, y_recv,
 ):
     x, core, y, z = place()
@@ -487,9 +487,9 @@
     def gather(o, to):
         def some(i, carry):
             for u in range(16):
-                at = idx[o * 512 + i * 16 + u]
+                n = o * 512 + i * 16 + u
                 to[pl.ds(i * 16 + u, 1), :] = (
-                    acc_s[pl.ds(at & 4095, 1), :] + acc_t[pl.ds(at >> 12, 1), :]
+                    acc_s[pl.ds(at_s[n], 1), :] + acc_t[pl.ds(at_t[n], 1), :]
                 )
             return carry
 
@@ -588,14 +588,14 @@
         c.wait_send()
 
 
-def finish(idx, acc_s, acc_t, rk_all, both, r_rows):
+def finish(at_s, at_t, acc_s, acc_t, rk_all, both, r_rows):
     vm = pl.BlockSpec(memory_space=pltpu.VMEM)
     hbm = pl.BlockSpec(memory_space=pltpu.HBM)
     dma = pltpu.SemaphoreType.DMA
     return pl.pallas_call(
         finish_kernel,
         out_shape=jax.ShapeDtypeStruct((32, CAP, W), BF16),
-        in_specs=[pl.BlockSpec(memory_space=pltpu.SMEM), vm, vm, vm, vm, hbm],
+        in_specs=[pl.BlockSpec(memory_space=pltpu.SMEM)] * 2 + [vm] * 4 + [hbm],
         out_specs=hbm,
         scratch_shapes=[
             pltpu.VMEM((4, ROWS_G, W), F32),
@@ -611,7 +611,7 @@
             collective_id=1, has_side_effects=True, vmem_limit_bytes=24 << 20
         ),
         name="finish",
-    )(idx, acc_s, acc_t, rk_all, both, pltpu.with_memory_space_constraint(r_rows, pltpu.HBM))
+    )(at_s, at_t, acc_s, acc_t, rk_all, both, pltpu.with_memory_space_constraint(r_rows, pltpu.HBM))
 
 
 def body(r_rows, r_keys, r_counts, s_rows, s_keys, s_counts, t_rows, t_keys, t_counts):
@@ -625,8 +625,7 @@
     a, b = kv >> 6, kv & 63
     at_s = (b & 3) * 1024 + (b >> 2) * 64 + a
     at_t = (a & 3) * 1024 + (a >> 2) * 64 + b
-    idx = (at_s + at_t * 4096).reshape(4096)
-    joined = finish(idx, acc_s, acc_t, rk_all, both, r_rows.reshape(32, CAP, W))
+    joined = finish(at_s.reshape(4096), at_t.reshape(4096), acc_s, acc_t, rk_all, both, r_rows.reshape(32, CAP, W))
     return joined.reshape(512, W)
 
 

time: 68.6 us -> 69 us (level)
  Pallas kernels: 66.8 us -> 67.5 us
    pallas_call x1, Pallas kernels: 26.2 us -> 26.9 us  [finish(): pl.pallas_call(finish_kernel, out_shape=jax.ShapeDtypeStruct((32, CAP, W)...]
where the time goes in v5:
time: 69 us; the launch traced here: 68.2 us
  Pallas kernels  67.5 us (98%)
    pallas_call x1, Pallas kernels, dispatch(): pl.pallas_call(dispatch_kernel, out_shape=out, in_specs=[pl.BlockSpec(mem...  40.2 us
    pallas_call x1, Pallas kernels, finish(): pl.pallas_call(finish_kernel, out_shape=jax.ShapeDtypeStruct((32, CAP, W)...  26.9 us

profile of v5, /device:TPU:1, one launch (start us, length us, event | category | flops | bytes accessed | tf_op | source)
XLA Modules:
  0.0 68.2 jit_solution(10616001827278224520)
XLA Ops:
  0.0 40.2 %dispatch.1 = (f32[4096,128]{1,0:T(8,128)S(1)}, f32[4096,128]{1,0:T(8,128)S(1)}, bf16[8,32,16,128]{3,2,1,0:T(8,128)(2,1)S(1)}, bf16[4,64,16,128]{3,2,1,0:T(8,128...) custom-call(bf16[32,16,128]{2,1,0:T(8,128)(2,1)} %bitcast.17, ...), custom_call_target="tpu_custom_call" | custom-call | tf_op jit(solution)/shard_map/dispatch/pallas_call | solution.py:373
  40.3 0.3 repair.1
  40.6 26.9 %finish.1 = bf16[32,16,128]{2,1,0:T(8,128)(2,1)S(1)} custom-call(s32[4096]{0:T(1024)S(1)} %bitcast.14, s32[4096]{0:T(1024)S(1)} %bitcast.13, f32[4096,128]{1,0:T(8,128)S(1)} %get-tuple-element.23.acc_s, f32[4096,128]{1,0:T(8,128)S(1)} %get-tuple-element.24.acc_t, s32[8,8,128]{2,1,0:T(8,128)S(1)} %get-tuple-element.15.rk_all, ...), custom_call_target="tpu_custom_call" | custom-call | tf_op jit(solution)/shard_map/finish/pallas_call | solution.py:595
  67.6 0.7 copy.16
  (1 shorter events, 0.0 us)
